TPU v7x, 32 devices: a whole 2x2x4 slice. The times are simulated.
32 devices in a mesh: seq: 2 (over x), shard: 16 (over z, y, core).
Axes of the slice: x: 2, y: 2, z: 4, core: 2. Of those that a mesh axis runs over, the one named last changes fastest.
Arguments:
- tokens: bfloat16 [32, 512, 1024], P(('seq', 'shard')), may hold values from -6 to 6
- cotangent: bfloat16 [32, 512, 1024], P(('seq', 'shard')), may hold values from -6 to 6
- lengths: int32 [16], replicated, may hold values from 512 to 1024, as said below
- first_gain: bfloat16 [1024], P('shard'), may hold values from 0.25 to 1.75
- first_bias: bfloat16 [1024], P('shard'), may hold values from -1.5 to 1.5
- qkv_weight: bfloat16 [1024, 3072], P('shard'), may hold values from -0.1875 to 0.1875
- qv_bias: bfloat16 [2048], P('shard'), may hold values from -1.5 to 1.5
- dense_weight: bfloat16 [1024, 1024], P('shard'), may hold values from -0.5 to 0.5
- dense_bias: bfloat16 [1024], P('shard'), may hold values from -1.5 to 1.5
- second_gain: bfloat16 [1024], P('shard'), may hold values from 0.25 to 1.75
- second_bias: bfloat16 [1024], P('shard'), may hold values from -1.5 to 1.5
- fc1_weight: bfloat16 [1024, 4096], P('shard'), may hold values from -0.1875 to 0.1875
- fc1_bias: bfloat16 [4096], P('shard'), may hold values from -1.5 to 1.5
- fc2_weight: bfloat16 [4096, 1024], P('shard'), may hold values from -0.09375 to 0.09375
- fc2_bias: bfloat16 [1024], P('shard'), may hold values from -1.5 to 1.5
Outputs:
- block_out: bfloat16 [32, 512, 1024], P(('seq', 'shard'))
- tokens_grad: bfloat16 [32, 512, 1024], P(('seq', 'shard'))
- first_gain_grad: float32 [1024], P('shard')
- first_bias_grad: float32 [1024], P('shard')
- qkv_weight_grad: float32 [1024, 3072], P('shard')
- qv_bias_grad: float32 [2048], P('shard')
- dense_weight_grad: float32 [1024, 1024], P('shard')
- dense_bias_grad: float32 [1024], P('shard')
- second_gain_grad: float32 [1024], P('shard')
- second_bias_grad: float32 [1024], P('shard')
- fc1_weight_grad: float32 [1024, 4096], P('shard')
- fc1_bias_grad: float32 [4096], P('shard')
- fc2_weight_grad: float32 [4096, 1024], P('shard')
- fc2_bias_grad: float32 [1024], P('shard')
Inputs may be any that keep to these rules, and one draw needn't show every extreme that they name: Every length is a multiple of 32; the lengths of each group's 1 sequence sum to at most 1024, and in some group to exactly 1024.
All inputs are finite; a program needn't handle non-finite values.
Results may differ from a plain program's by a relative error of at most 0.019.
Values may be sent and summed in bfloat16 or wider, within the bound.
A program may use at most 192 MiB of HBM per device.

v0:
```python
import functools

import jax
import jax.numpy as jnp
import numpy as np
from jax import lax
from jax.experimental import pallas as pl
from jax.experimental.pallas import tpu as pltpu
from jax.sharding import PartitionSpec as P

HEADS = 16
HEAD = 64
ROWS = 8

epsilon = 1e-05
masked_score = -1e30
f32 = jnp.float32
bf16 = jnp.bfloat16


def gelu_tanh(values):
    return (
        0.5
        * values
        * (1.0 + jnp.tanh(0.7978845608028654 * (values + 0.044715 * values * values * values)))
    )


def normalize(hidden):
    center = hidden - jnp.mean(hidden, axis=-1, keepdims=True)
    spread = jnp.mean(center * center, axis=-1, keepdims=True)
    root = lax.rsqrt(spread + epsilon)
    return center * root, root


def norm_pull(grad, gain, xhat, root):
    scaled = grad * gain
    return root * (
        scaled
        - jnp.mean(scaled, axis=-1, keepdims=True)
        - xhat * jnp.mean(scaled * xhat, axis=-1, keepdims=True)
    )


def slot_ids(first, count, lanes):
    place = first + lax.broadcasted_iota(jnp.int32, (count, 1), 0)
    block, inside = place // (ROWS * lanes), place % (ROWS * lanes)
    return (block * ROWS + inside % ROWS) * lanes + inside // ROWS


def blocked_ids(shape, axis, lanes):
    place = lax.broadcasted_iota(jnp.int32, shape, axis)
    high = (ROWS * lanes).bit_length() - 1
    inside = place & (ROWS * lanes - 1)
    row = (place >> high) * ROWS + (inside & (ROWS - 1))
    return (row * lanes + (inside >> (ROWS.bit_length() - 1))).astype(f32)


def attn_mask(scored, allowed):
    return jnp.where(allowed, scored, masked_score)


def attn_fwd_kernel(lanes, tile, one_seq, slope_ref, idc_ref, idr_ref, beginc_ref, q_ref, k_ref, v_ref, o_ref):
    tokens = q_ref.shape[0]
    block = ROWS * lanes
    lane_id = lax.broadcasted_iota(jnp.int32, (1, 2 * HEAD), 1)
    for b in range(tokens // block):
        end = (b + 1) * block

        def step(t, _):
            at = pl.ds(pl.multiple_of(b * block + t * tile, tile), tile)
            q = q_ref[at, :] * jnp.asarray(HEAD**-0.5, bf16)
            ids_q = idc_ref[at, :]
            both = None
            for j in range(2):
                mine = (lane_id // HEAD) == j
                qj = jnp.where(mine, q, jnp.zeros_like(q))
                s = lax.dot_general(
                    qj, k_ref[:end, :], (((1,), (1,)), ((), ())), preferred_element_type=f32
                )
                s = s + slope_ref[0, 0, j] * idr_ref[:, :end]
                if one_seq:
                    own = s[:, b * block :]
                    own = attn_mask(own, idr_ref[:, b * block : end] <= ids_q)
                    s = jnp.concatenate([s[:, : b * block], own], axis=1) if b else own
                else:
                    ids_k = idr_ref[:, :end]
                    s = attn_mask(s, (ids_k <= ids_q) & (ids_k >= beginc_ref[at, :]))
                top = jnp.max(s, axis=1, keepdims=True)
                e = jnp.exp(s - top)
                total = jnp.sum(e, axis=1, keepdims=True)
                o = jnp.dot(e.astype(bf16), v_ref[:end, :], preferred_element_type=f32) / total
                both = o if both is None else jnp.where(mine, o, both)
            o_ref[at, :] = both.astype(bf16)
            return 0

        lax.fori_loop(0, block // tile, step, 0)


def attn_bwd_kernel(
    lanes, tile, one_seq, slope_ref, idc_ref, idr_ref, beginr_ref, q_ref, k_ref, v_ref, do_ref,
    dq_ref, dk_ref, dv_ref, dk_acc, dv_acc, bias_acc,
):
    tokens = q_ref.shape[0]
    block = ROWS * lanes
    lane_id = lax.broadcasted_iota(jnp.int32, (1, 2 * HEAD), 1)
    dk_acc[...] = jnp.zeros_like(dk_acc)
    dv_acc[...] = jnp.zeros_like(dv_acc)
    for j in range(2):
        bias_acc[j] = jnp.broadcast_to(slope_ref[0, 0, j] * idc_ref[...], (tokens, tile))
    for b in range(tokens // block):
        end = (b + 1) * block

        def step(t, _):
            at = pl.ds(pl.multiple_of(b * block + t * tile, tile), tile)
            q = q_ref[at, :] * jnp.asarray(HEAD**-0.5, bf16)
            do = do_ref[at, :]
            ids_q = idr_ref[:, at]
            both = None
            for j in range(2):
                mine = (lane_id // HEAD) == j
                qj = jnp.where(mine, q, jnp.zeros_like(q))
                doj = jnp.where(mine, do, jnp.zeros_like(do))
                s = lax.dot_general(
                    k_ref[:end, :], qj, (((1,), (1,)), ((), ())), preferred_element_type=f32
                )
                s = s + bias_acc[j, :end, :]
                if one_seq:
                    own = s[b * block :, :]
                    own = attn_mask(own, idc_ref[b * block : end, :] <= ids_q)
                    s = jnp.concatenate([s[: b * block, :], own], axis=0) if b else own
                else:
                    ids_k = idc_ref[:end, :]
                    s = attn_mask(s, (ids_k <= ids_q) & (ids_k >= beginr_ref[:, at]))
                top = jnp.max(s, axis=0, keepdims=True)
                e = jnp.exp(s - top)
                probs = e * (1.0 / jnp.sum(e, axis=0, keepdims=True))
                dv_acc[:end, :] += jnp.dot(probs.astype(bf16), doj, preferred_element_type=f32)
                dp = lax.dot_general(
                    v_ref[:end, :], doj, (((1,), (1,)), ((), ())), preferred_element_type=f32
                )
                inner = jnp.sum(probs * dp, axis=0, keepdims=True)
                ds = (probs * (dp - inner)).astype(bf16)
                dk_acc[:end, :] += jnp.dot(ds, qj, preferred_element_type=f32)
                dq = lax.dot_general(
                    ds, k_ref[:end, :], (((0,), (0,)), ((), ())), preferred_element_type=f32
                )
                both = dq if both is None else jnp.where(mine, dq, both)
            dq_ref[at, :] = (both * (HEAD**-0.5)).astype(bf16)
            return 0

        lax.fori_loop(0, block // tile, step, 0)
    dk_ref[...] = dk_acc[...].astype(bf16)
    dv_ref[...] = dv_acc[...].astype(bf16)


def attn_shape(tokens, width, lanes):
    pairs = width // (2 * HEAD)
    tile = min(256, ROWS * lanes)
    return pairs, tile


def attention_forward(qkv, slopes, ids, begins, lanes, one_seq):
    tokens, width = qkv.shape[0], qkv.shape[1] // 3
    pairs, tile = attn_shape(tokens, width, lanes)
    column = lambda part: pl.BlockSpec((tokens, 2 * HEAD), lambda h, part=part: (0, part * pairs + h))
    whole = lambda a: pl.BlockSpec(a.shape, lambda h: (0, 0))
    idc, idr, beginc = ids[:, None], ids[None, :], begins[:, None]
    half = tokens * tokens * 5 // 8
    return pl.pallas_call(
        functools.partial(attn_fwd_kernel, lanes, tile, one_seq),
        grid=(pairs,),
        in_specs=[
            pl.BlockSpec((1, 1, 2), lambda h: (h, 0, 0), memory_space=pltpu.SMEM),
            whole(idc), whole(idr), whole(beginc), column(0), column(1), column(2),
        ],
        out_specs=pl.BlockSpec((tokens, 2 * HEAD), lambda h: (0, h)),
        out_shape=jax.ShapeDtypeStruct((tokens, width), bf16),
        compiler_params=pltpu.CompilerParams(vmem_limit_bytes=48 * 2**20),
        cost_estimate=pl.CostEstimate(
            flops=8 * pairs * half * HEAD * 2, transcendentals=2 * pairs * half, bytes_accessed=8 * tokens * width
        ),
        name="attention_forward",
    )(slopes.reshape(pairs, 1, 2), idc, idr, beginc, qkv, qkv, qkv)


def attention_backward(qkv, grad_out, slopes, ids, begins, lanes, one_seq):
    tokens, width = grad_out.shape
    pairs, tile = attn_shape(tokens, width, lanes)
    column = lambda part: pl.BlockSpec((tokens, 2 * HEAD), lambda h, part=part: (0, part * pairs + h))
    whole = lambda a: pl.BlockSpec(a.shape, lambda h: (0, 0))
    idc, idr, beginr = ids[:, None], ids[None, :], begins[None, :]
    plane = lambda part: pl.BlockSpec((None, tokens, 2 * HEAD), lambda h, part=part: (part * pairs + h, 0, 0))
    out = jax.ShapeDtypeStruct((tokens, width), bf16)
    half = tokens * tokens * 5 // 8
    return pl.pallas_call(
        functools.partial(attn_bwd_kernel, lanes, tile, one_seq),
        grid=(pairs,),
        in_specs=[
            pl.BlockSpec((1, 1, 2), lambda h: (h, 0, 0), memory_space=pltpu.SMEM),
            whole(idc), whole(idr), whole(beginr), plane(0), plane(1), plane(2), column(0),
        ],
        out_specs=[column(0)] * 3,
        out_shape=[out] * 3,
        scratch_shapes=[
            pltpu.VMEM((tokens, 2 * HEAD), f32), pltpu.VMEM((tokens, 2 * HEAD), f32), pltpu.VMEM((2, tokens, tile), f32),
        ],
        compiler_params=pltpu.CompilerParams(vmem_limit_bytes=56 * 2**20),
        cost_estimate=pl.CostEstimate(
            flops=20 * pairs * half * HEAD * 2, transcendentals=2 * pairs * half, bytes_accessed=14 * tokens * width
        ),
        name="attention_backward",
    )(slopes.reshape(pairs, 1, 2), idc, idr, beginr, qkv, qkv, qkv, grad_out)


def take(blocks, index, axis=0):
    return lax.dynamic_index_in_dim(blocks, index, axis, keepdims=False)


def seq_gather(block, axis):
    n, me = lax.axis_size("seq"), lax.axis_index("seq")
    shape = block.shape[:axis] + (n,) + block.shape[axis:]
    if n == 2:
        peer = lax.ppermute(block, "seq", [(0, 1), (1, 0)])
        return jnp.where(me == 0, jnp.stack([block, peer], axis), jnp.stack([peer, block], axis))
    whole = lax.dynamic_update_index_in_dim(jnp.zeros(shape, block.dtype), block, me, axis)
    for d in range(1, n):
        got = lax.ppermute(block, "seq", [(i, (i + d) % n) for i in range(n)])
        whole = lax.dynamic_update_index_in_dim(whole, got, (me - d) % n, axis)
    return whole


def seq_blocks(whole, axis, dtype):
    n, me = lax.axis_size("seq"), lax.axis_index("seq")
    got = [take(whole, me, axis)]
    for d in range(1, n):
        sent = take(whole, (me + d) % n, axis).astype(dtype)
        got.append(lax.ppermute(sent, "seq", [(i, (i + d) % n) for i in range(n)]))
    return got


def seq_sum(whole, axis, dtype=bf16):
    got = seq_blocks(whole, axis, dtype)
    return sum((g.astype(f32) for g in got[1:]), got[0].astype(f32))


def shard_factors(n):
    nc = 2 if n % 2 == 0 else 1
    nz = 4 if n % (4 * nc) == 0 else 1
    return nz, n // (nz * nc), nc


def shard_reduce(blocks, dtype):
    n, me = lax.axis_size("shard"), lax.axis_index("shard")
    sizes = shard_factors(n)
    blocks = blocks.reshape(sizes + blocks.shape[1:])
    place = (me // (sizes[1] * sizes[2]), me // sizes[2] % sizes[1], me % sizes[2])
    strides = (sizes[1] * sizes[2], sizes[2], 1)
    for axis in (2, 1, 0):
        size, mine, stride = sizes[axis], place[axis], strides[axis]
        total = take(blocks, mine, axis).astype(f32)
        for d in range(1, size):
            sent = take(blocks, (mine + d) % size, axis).astype(dtype)
            pairs = [
                (i, i - (i // stride % size) * stride + ((i // stride % size + d) % size) * stride)
                for i in range(n)
            ]
            total = total + lax.ppermute(sent, "shard", pairs).astype(f32)
        blocks = total if axis == 0 else total.astype(dtype)
    return blocks


MESH = pl.DeviceIdType.MESH


class Geometry:
    def __init__(self, seqs, shards):
        self.seqs, self.shards = seqs, shards
        self.sizes = shard_factors(shards)
        self.s, self.k = lax.axis_index("seq"), lax.axis_index("shard")
        nz, ny, nc = self.sizes
        self.z, self.y, self.c = self.k // (ny * nc), self.k // nc % ny, self.k % nc
        self.inner = (self.z + 1) // 2 % 2
        high = self.z // 2
        self.line = (self.z, self.z + 1 - 2 * (self.z % 2), 2 - high, 3 - 3 * high)

    def slot(self, i, dy, dc):
        nz, ny, nc = self.sizes
        return (self.line[i] * ny + (self.y + dy) % ny) * nc + (self.c + dc) % nc


class Wires:
    def __init__(self, geometry, send_sems, recv_sems):
        self.g, self.send_sems, self.recv_sems = geometry, send_sems, recv_sems
        self.sends, self.used = [], 0

    def block(self, count):
        first = self.used
        self.used += count
        return first

    def copy(self, src, dst, sent, got, s, k):
        return pltpu.make_async_remote_copy(
            src_ref=src, dst_ref=dst, send_sem=self.send_sems.at[sent], recv_sem=self.recv_sems.at[got],
            device_id={"seq": s, "shard": k}, device_id_type=MESH,
        )

    def send_as(self, src, dst, sent, got, s, k, like):
        self.copy(src, dst, sent, got, s, k).start()
        self.sends.append((like, sent))

    def recorded(self, like, index):
        self.sends.append((like, index))

    def send(self, src, dst, index, s, k, like):
        self.send_as(src, dst, index, index, s, k, like)

    def arrived(self, dst, index):
        self.copy(dst, dst, index, index, 1 - self.g.s, self.g.k).wait_recv()

    def drain(self):
        for like, index in self.sends:
            self.copy(like, like, index, index, 1 - self.g.s, self.g.k).wait_send()
        self.sends = []


def enter(geometry):
    g = geometry
    barrier = pltpu.get_barrier_semaphore()
    for d in range(1, g.shards):
        pl.semaphore_signal(
            barrier, inc=1, device_id={"seq": g.s, "shard": (g.k + d) % g.shards}, device_id_type=MESH
        )
    pl.semaphore_signal(barrier, inc=1, device_id={"seq": 1 - g.s, "shard": g.k}, device_id_type=MESH)
    pl.semaphore_wait(barrier, g.shards)


class Gather:
    def __init__(self, wires, own, out):
        self.w, self.g, self.own, self.out = wires, wires.g, own, out
        nz, ny, nc = self.g.sizes
        self.z0 = wires.block(nz)
        self.on0 = wires.block(nz)
        self.y0 = wires.block(nz * ny)
        self.c0 = wires.block(nz * ny * nc)

    def on_y(self, i, src):
        g = self.g
        for dy in range(1, g.sizes[1]):
            self.w.send(src, self.out.at[g.slot(i, 0, 0)], self.y0 + i * g.sizes[1] + dy, g.s, g.slot(0, dy, 0), self.own)

    def on_core(self, i, dy, src):
        g = self.g
        for dc in range(1, g.sizes[2]):
            index = self.c0 + (i * g.sizes[1] + dy) * g.sizes[2] + dc
            self.w.send(src, self.out.at[g.slot(i, -dy, 0)], index, g.s, g.slot(0, 0, dc), self.own)

    def start(self):
        g = self.g
        here = self.out.at[g.k]
        self.w.send_as(self.own, here, self.z0 + 2, self.z0 + 3 - g.inner, g.s, g.slot(2, 0, 0), self.own)
        self.w.send(self.own, here, self.z0 + 1, g.s, g.slot(1, 0, 0), self.own)

    def start_near(self):
        self.on_y(0, self.own)
        self.on_core(0, 0, self.own)

    def poll_z(self):
        g = self.g
        for i in (1, 2, 3):
            at = self.out.at[g.slot(i, 0, 0)]
            self.w.arrived(at, self.z0 + i)
            if i > 1:

                @pl.when(g.inner == 1)
                def _(at=at, i=i):
                    self.w.copy(at, at, self.on0 + i, self.z0 + i, g.s, g.slot(1, 0, 0)).start()

            self.on_y(i, at)
            self.on_core(i, 0, at)

    def poll_y(self):
        g = self.g
        for i in range(g.sizes[0]):
            for dy in range(1, g.sizes[1]):
                at = self.out.at[g.slot(i, -dy, 0)]
                self.w.arrived(at, self.y0 + i * g.sizes[1] + dy)
                self.on_core(i, dy, at)

    def finish(self):
        g = self.g
        for i in range(g.sizes[0]):
            for dy in range(g.sizes[1]):
                for dc in range(1, g.sizes[2]):
                    at = self.out.at[g.slot(i, -dy, -dc)]
                    self.w.arrived(at, self.c0 + (i * g.sizes[1] + dy) * g.sizes[2] + dc)

        @pl.when(g.inner == 1)
        def _():
            for i in (2, 3):
                self.w.copy(self.own, self.own, self.on0 + i, self.z0 + i, g.s, g.k).wait_send()


class Tokens:
    def __init__(self, wires, packed, out):
        self.w, self.g, self.packed, self.out = wires, wires.g, packed, out
        self.blocks = out.shape[0]
        self.at = wires.block((self.g.shards + 1) * self.blocks)
        self.like, self.row = packed.at[0, 0], packed.at[:, 0]

    def index(self, b, d):
        return self.at + b * (self.g.shards + 1) + d

    def mine(self, b, s):
        return self.out.at[b, pl.ds(pl.multiple_of(s * self.g.shards, self.g.shards), self.g.shards)]

    def start(self, b):
        g = self.g
        for d in range(1, g.shards):
            to = (g.k + d) % g.shards
            lane = self.out.at[b, g.s * g.shards + g.k]
            self.w.send(self.packed.at[to, b], lane, self.index(b, d), g.s, to, self.like)

    def poll(self, b):
        g = self.g
        for d in range(1, g.shards):
            self.w.arrived(self.out.at[b, g.s * g.shards + (g.k - d) % g.shards], self.index(b, d))
        self.w.send(self.mine(b, g.s), self.mine(b, g.s), self.index(b, g.shards), 1 - g.s, g.k, self.row)

    def finish(self, b):
        self.w.arrived(self.mine(b, 1 - self.g.s), self.index(b, self.g.shards))


class Smalls:
    def __init__(self, wires, held, at):
        self.w, self.g, self.held, self.at = wires, wires.g, held, at

    def start(self):
        g = self.g
        mine = self.held.at[g.k]
        for d in range(1, g.shards):
            self.w.send(mine, mine, self.at + d, g.s, (g.k + d) % g.shards, mine)

    def finish(self):
        g = self.g
        for d in range(1, g.shards):
            self.w.arrived(self.held.at[(g.k - d) % g.shards], self.at + d)


def side_by_side(vec, small, row, to, count):
    for j in range(small.shape[0]):
        vec[to : to + 1, j * count : (j + 1) * count] = small[j, row : row + 1, :count]


def forward_kernel(
    seqs, shards, counts,
    packed, packed_cot, qkv_w, small, dense_w, fc1_w, fc2_w, slopes, lengths,
    x_out, cot_out, n1_out, n2_out, qkvw_out, dense_out, fc1_out, fc2_out, qkv_out, o_out, h2_out, a_out, slope_out,
    w2_out, vec_out,
    x_v, n1_v, n2_v, qkvw_v, small_v, dense_v, fc1_v, fc2_v, blocks_v, cot_v, qkv_v, o_v, h2_v, a_v, slope_v, w2_v, vec_v, idc, idr,
    send_sems, recv_sems, copy_sems,
):
    g = Geometry(seqs, shards)
    wires = Wires(g, send_sems, recv_sems)
    lanes = seqs * shards
    width = n1_v.shape[1]
    part = o_v.shape[2]
    pairs = part // (2 * HEAD)
    ff = fc1_v.shape[2]
    ff_part = ff // shards
    block = ROWS * lanes
    blocks = x_v.shape[0]
    half = block // seqs
    rows = width // shards
    local = []

    def bring(src, dst):
        made = pltpu.make_async_copy(src, dst, copy_sems.at[len(local)])
        made.start()
        local.append(made)
        return made

    def at_block(b):
        return pl.ds(pl.multiple_of(b * block, block), block)

    tokens = Tokens(wires, packed, x_v)
    cots = Tokens(wires, packed_cot, blocks_v)
    smalls_at = wires.block(shards)
    qkv_all = Gather(wires, qkvw_v.at[g.k], qkvw_v)
    dense_all = Gather(wires, dense_v.at[g.k], dense_v)
    up_all = Gather(wires, fc1_v.at[g.k], fc1_v)
    down_all = Gather(wires, fc2_v, fc2_out)
    heads_at = wires.block(blocks)

    staged_qkv = [
        bring(
            qkv_w.at[:, pl.ds(pl.multiple_of(p * width + g.s * part, 128), part)],
            qkvw_v.at[g.k, :, pl.ds(p * part, part)],
        )
        for p in range(3)
    ]
    staged_small = bring(small, small_v.at[g.k])
    staged_dense = bring(dense_w, dense_v.at[g.k])
    staged_up = [
        bring(
            fc1_w.at[:, pl.ds(pl.multiple_of((i * seqs + g.s) * ff_part, 128), ff_part)],
            fc1_v.at[g.k, :, pl.ds(i * ff_part, ff_part)],
        )
        for i in range(shards)
    ]
    staged_x = bring(packed.at[g.k], x_v.at[:, g.s * shards + g.k])
    staged_down = bring(fc2_w.at[pl.ds(pl.multiple_of(g.s * ff_part, 8), ff_part), :], fc2_v)
    staged_cot = bring(packed_cot.at[g.k], blocks_v.at[:, g.s * shards + g.k])
    enter(g)
    idc[...] = blocked_ids(idc.shape, 0, lanes)
    idr[...] = blocked_ids(idr.shape, 1, lanes)
    for made in staged_qkv:
        made.wait()
    staged_small.wait()
    staged_dense.wait()
    for made in staged_up:
        made.wait()
    staged_down.wait()
    staged_x.wait()
    staged_cot.wait()
    kept = [bring(fc2_v, fc2_out.at[g.k])]
    smalls = Smalls(wires, small_v, smalls_at)
    qkv_all.start()
    qkv_all.start_near()
    tokens.start(0)
    tokens.start(1)
    smalls.start()
    dense_all.start_near()
    up_all.start_near()
    down_all.start_near()
    tokens.poll(0)
    tokens.start(2)
    qkv_all.poll_z()
    tokens.poll(1)
    tokens.start(3)
    dense_all.start()
    up_all.start()
    smalls.finish()

    for row in (0, 1, 3, 4, 5, 7):
        side_by_side(vec_v, small_v, row, row, rows)
    vec_v[2:3, :] = jnp.zeros((1, vec_v.shape[1]), f32)
    per = 2 * width // shards
    for i in range(part // per):
        for row, side in ((0, 0), (2, 1)):
            j = (side * width + g.s * part) // per + i
            vec_v[2:3, row * part + i * per : row * part + (i + 1) * per] = small_v[j, 2:3, :per]
    for j in range(shards):
        vec_v[6:7, j * ff_part : (j + 1) * ff_part] = small_v[j, 6:7, pl.ds(pl.multiple_of(g.s * ff_part, 128), ff_part)]

    qkv_all.poll_y()
    tokens.poll(2)
    tokens.poll(3)
    down_all.start()
    qkv_all.finish()
    kept += [bring(qkvw_v, qkvw_out), bring(vec_v, vec_out)]

    lane_id = lax.broadcasted_iota(jnp.int32, (1, 2 * HEAD), 1)
    tile = min(256, block)

    def project(b):
        x = x_v[b].astype(f32).reshape(block, width)
        xhat, _ = normalize(x)
        n1 = (xhat * vec_v[0:1, :width] + vec_v[1:2, :width]).astype(bf16)
        at = at_block(b)
        n1_v[at, :] = n1
        for p in range(3):
            weight = qkvw_v[:, :, p * part : (p + 1) * part].reshape(width, part)
            out = jnp.dot(n1, weight, preferred_element_type=f32) + vec_v[2:3, p * part : (p + 1) * part]
            out = out.astype(bf16)
            for h in range(pairs):
                qkv_v[p * pairs + h, at, :] = out[:, h * 2 * HEAD : (h + 1) * 2 * HEAD]

    def attend(b):
        end = (b + 1) * block

        @pl.loop(0, pairs)
        def _(h):
            q_ref, k_ref, v_ref = qkv_v.at[h], qkv_v.at[pairs + h], qkv_v.at[2 * pairs + h]
            for t in range(block // tile):
                at = pl.ds(b * block + t * tile, tile)
                q = q_ref[at, :] * jnp.asarray(HEAD**-0.5, bf16)
                ids_q = idc[at, :]

                def one_head(j, both):
                    mine = (lane_id >= HEAD).astype(jnp.int32) == j
                    qj = jnp.where(mine, q, jnp.zeros_like(q))
                    s = lax.dot_general(
                        qj, k_ref[:end, :], (((1,), (1,)), ((), ())), preferred_element_type=f32
                    )
                    s = s + slopes[g.s * pairs + h, j] * idr[:, :end]
                    tail = attn_mask(s[:, b * block :], idr[:, b * block : end] <= ids_q)
                    s = jnp.concatenate([s[:, : b * block], tail], axis=1) if b else tail
                    top = jnp.max(s, axis=1, keepdims=True)
                    e = jnp.exp(s - top)
                    total = jnp.sum(e, axis=1, keepdims=True)
                    o = jnp.dot(e.astype(bf16), v_ref[:end, :], preferred_element_type=f32) / total
                    return jnp.where(mine, o, both)

                both = lax.fori_loop(0, 2, one_head, jnp.zeros((tile, 2 * HEAD), f32))
                o_v[g.s, at, pl.ds(pl.multiple_of(h * 2 * HEAD, 2 * HEAD), 2 * HEAD)] = both.astype(bf16)

    def head_copy(b):
        mine = o_v.at[g.s, at_block(b)]
        return wires.copy(mine, mine, heads_at + b, heads_at + b, 1 - g.s, g.k)

    for b in range(blocks):
        tokens.finish(b)
        project(b)
        attend(b)
        head_copy(b).start()
        if b == 0:
            dense_all.poll_z()
        if b == 1:
            up_all.poll_z()
        if b == 2:
            dense_all.poll_y()
            cots.start(0)
            cots.start(1)
        if b == 3:
            up_all.poll_y()
    kept += [bring(x_v, x_out), bring(n1_v, n1_out), bring(qkv_v, qkv_out)]
    down_all.poll_z()
    dense_all.finish()
    kept.append(bring(dense_v, dense_out))
    up_all.finish()
    kept.append(bring(fc1_v, fc1_out))

    @pl.loop(0, blocks)
    def _(b):
        at = at_block(b)
        wires.arrived(o_v.at[1 - g.s, at], heads_at + b)
        branch = jnp.dot(
            o_v[0, at, :], dense_v[: shards // 2].reshape(part, width), preferred_element_type=f32
        ) + jnp.dot(o_v[1, at, :], dense_v[shards // 2 :].reshape(part, width), preferred_element_type=f32)
        resid = x_v[b].astype(f32).reshape(block, width) + branch + vec_v[3:4, :width]
        h2_v[b] = jnp.where(g.s == 0, resid[:half], resid[half:])
        xhat, _ = normalize(resid)
        n2 = (xhat * vec_v[4:5, :width] + vec_v[5:6, :width]).astype(bf16)
        n2_v[at, :] = n2
        step = min(512, ff)

        @pl.loop(0, ff // step)
        def _(n):
            cut = pl.ds(pl.multiple_of(n * step, step), step)
            u = jnp.dot(n2_v[at, :], fc1_v[:, :, cut].reshape(width, step), preferred_element_type=f32) + vec_v[6:7, cut]
            inside = 0.7978845608028654 * u * (1.0 + 0.044715 * u * u)
            t = jnp.tanh(inside)
            a_v[at, cut] = (0.5 * u * (1.0 + t)).astype(bf16)
            slope = 0.5 * (1.0 + t) + 0.5 * u * (1.0 - t * t) * (
                0.7978845608028654 + (0.7978845608028654 * 3.0 * 0.044715) * u * u
            )
            slope_v[at, cut] = slope.astype(bf16)

        @pl.when(b == 0)
        def _():
            cots.poll(0)
            cots.start(2)

        @pl.when(b == 1)
        def _():
            cots.poll(1)
            cots.start(3)

        @pl.when(b == 2)
        def _():
            cots.poll(2)


    cots.poll(3)
    kept.append(bring(o_v, o_out))
    kept += [bring(n2_v, n2_out), bring(h2_v, h2_out), bring(a_v, a_out), bring(slope_v, slope_out)]
    down_all.poll_y()
    for b in range(blocks):
        cots.finish(b)

    @pl.loop(0, blocks)
    def _(b):
        at = at_block(b)
        grad = blocks_v[b].astype(f32).reshape(block, width)
        cot_v[at, :] = jnp.where(idc[at, :] < lengths[g.k].astype(f32), grad, 0.0).astype(bf16)

    kept.append(bring(cot_v, cot_out))

    @pl.loop(0, ff // (2 * ff_part))
    def _(m):
        cut = a_v[:, pl.ds(pl.multiple_of(m * 2 * ff_part, 128), 2 * ff_part)]
        out = lax.dot_general(cut, cot_v[...], (((0,), (0,)), ((), ())), preferred_element_type=f32).astype(bf16)
        w2_v[pl.ds(2 * m, 2)] = out.reshape(2, ff_part, width)

    kept.append(bring(w2_v, w2_out))
    down_all.finish()
    for b in range(blocks):
        head_copy(b).wait_send()
    wires.drain()
    for made in kept:
        made.wait()
    assert wires.used <= counts[0] and len(local) <= counts[1]


def forward_exchange(packed, packed_cot, qkv_w, small, dense_w, fc1_w, fc2_w, slopes, lengths, seqs, shards):
    width, own = qkv_w.shape[0] * shards, qkv_w.shape[0]
    lanes = seqs * shards
    blocks = packed.shape[1]
    block = lanes * ROWS
    cap = blocks * block
    part = width // seqs
    pairs = part // (2 * HEAD)
    ff = fc1_w.shape[1] // seqs
    ff_part = ff // shards
    counts = (384, 64)
    any_ = pl.BlockSpec(memory_space=pl.ANY)
    vmem = pl.BlockSpec(memory_space=pltpu.VMEM)
    smem = pl.BlockSpec(memory_space=pltpu.SMEM)
    x_shape = ((blocks, lanes, ROWS, width), bf16)
    wide, long = ((cap, width), bf16), ((cap, ff), bf16)
    qkvw, dense, fc1, fc2 = (
        ((shards,) + tail, bf16) for tail in ((own, 3 * part), (own, width), (own, ff), (ff_part, width))
    )
    qkv, heads = ((3 * pairs, cap, 2 * HEAD), bf16), ((seqs, cap, part), bf16)
    h2, vec = ((blocks, block // seqs, width), f32), ((8, max(width, 3 * part, ff)), f32)
    outs = [x_shape, wide, wide, wide, qkvw, dense, fc1, fc2, qkv, heads, h2, long, long, fc2, vec]
    scratch = [
        x_shape, wide, wide, qkvw, ((shards,) + small.shape, f32), dense, fc1, ((ff_part, width), bf16), x_shape, wide,
        qkv, heads, h2, long, long, fc2, vec, ((cap, 1), f32), ((1, cap), f32),
    ]
    return pl.pallas_call(
        functools.partial(forward_kernel, seqs, shards, counts),
        in_specs=[any_] * 7 + [smem] * 2,
        out_specs=[any_] * len(outs),
        out_shape=[jax.ShapeDtypeStruct(s, d) for s, d in outs],
        scratch_shapes=[pltpu.VMEM(s, d) for s, d in scratch]
        + [pltpu.SemaphoreType.DMA((counts[0],)), pltpu.SemaphoreType.DMA((counts[0],)), pltpu.SemaphoreType.DMA((counts[1],))],
        compiler_params=pltpu.CompilerParams(collective_id=1, has_side_effects=True, vmem_limit_bytes=60 * 2**20),
        name="forward_exchange",
    )(
        packed, packed_cot, qkv_w, small, dense_w, fc1_w, fc2_w, slopes, lengths,
    )


class Scatter:
    def __init__(self, wires, full, own, bufs):
        self.w, self.g, self.full, self.own = wires, wires.g, full, own
        self.rc, self.ry, self.rz, self.fin = bufs
        self.at = wires.block(8)
        self.one = self.rz.at[0] if self.rz is not None else None

    def add(self, count, into, other):
        @pl.loop(0, count)
        def _(i):
            a, b = into(i), other(i)
            a[...] = (a[...].astype(f32) + b[...].astype(f32)).astype(bf16)

    def core_send(self):
        g = self.g
        self.w.send(self.full.at[:, :, 1 - g.c], self.rc, self.at, g.s, g.slot(0, 0, 1), self.rc)

    def core_done(self):
        g = self.g
        self.w.arrived(self.rc, self.at)
        self.add(8, lambda i: self.rc.at[i // 2, i % 2], lambda i: self.own(i // 2, i % 2))
        self.w.send(self.rc.at[:, 1 - g.y], self.ry, self.at + 1, g.s, g.slot(0, 1, 0), self.ry)

    def y_done(self):
        g = self.g
        self.w.arrived(self.ry, self.at + 1)
        self.add(4, lambda i: self.ry.at[i], lambda i: self.rc.at[i, g.y])

    def z_send(self):
        g = self.g
        partner = g.slot(1, 0, 0)
        self.w.send(self.ry.at[g.line[1]], self.rz.at[0], self.at + 2, g.s, partner, self.one)

        @pl.when(g.inner == 0)
        def _():
            for i in (2, 3):
                self.w.copy(self.ry.at[g.line[i]], self.rz.at[i], self.at + 1 + i, self.at + 1 + i, g.s, partner).start()

    def z_done(self):
        g = self.g

        @pl.when(g.inner == 1)
        def _():
            for i in (2, 3):
                self.w.arrived(self.rz.at[i], self.at + 1 + i)
                a = self.rz.at[i]
                a[...] = (a[...].astype(f32) + self.ry[g.line[i]].astype(f32)).astype(bf16)
                self.w.copy(a, self.rz.at[1], self.at + 1 + i, self.at + 5, g.s, g.slot(i, 0, 0)).start()

    def final(self):
        g = self.g
        self.w.arrived(self.rz.at[0], self.at + 2)
        self.w.arrived(self.rz.at[1], self.at + 5)
        total = self.ry[g.z].astype(f32) + self.rz[0].astype(f32) + self.rz[1].astype(f32)
        self.fin[0] = total.astype(bf16)
        self.w.send(self.fin.at[0], self.fin.at[1], self.at + 6, 1 - g.s, g.k, self.fin.at[0])

    def done(self):
        self.w.arrived(self.fin.at[1], self.at + 6)
        for i in (2, 3):
            self.w.copy(self.fin.at[0], self.fin.at[0], self.at + 1 + i, self.at + 1 + i, self.g.s, self.g.k).wait_send()


class Back:
    def __init__(self, wires, src, dst, pieces):
        self.w, self.g, self.src, self.dst, self.pieces = wires, wires.g, src, dst, pieces
        self.at = wires.block(wires.g.shards * pieces)
        self.per = src.shape[0] // pieces
        self.like = src.at[pl.ds(0, self.per), 0]

    def cut(self, ref, i):
        return ref.at[pl.ds(i * self.per, self.per)]

    def send(self, i):
        g = self.g
        for d in range(1, g.shards):
            to = (g.k + d) % g.shards
            src = self.src.at[pl.ds(i * self.per, self.per), to]
            index = self.at + i * g.shards + d
            self.w.copy(src, self.cut(self.dst.at[g.k], i), index, index, g.s, to).start()

    def finish(self):
        g = self.g
        for i in range(self.pieces):
            for d in range(1, g.shards):
                self.w.recorded(self.like, self.at + i * g.shards + d)
                self.w.arrived(self.cut(self.dst.at[(g.k - d) % g.shards], i), self.at + i * g.shards + d)


def middle_kernel(
    seqs, shards, counts,
    a, slope, n2, fc1, fc2, dense, cot, h2, heads, w2, vec,
    dh2_out, do_out, w1_out, wd_out, keep_out, give_out, ry_out, small_out,
    a_v, du_v, n2_v, fc1_v, fc2_v, dense_v, cot_v, h2_v, heads_v, own_w2, w1_v, wd_v, mine_v, sent_v, got_v,
    da_v, do_v, do_sent, small_v, rc, ry,
    send_sems, recv_sems, copy_sems,
):
    g = Geometry(seqs, shards)
    wires = Wires(g, send_sems, recv_sems)
    blocks, half, width = h2_v.shape
    block = half * seqs
    ff = a_v.shape[1]
    ff_part = ff // shards
    rows = width // shards
    part = width // seqs
    local = []

    def bring(src, dst):
        made = pltpu.make_async_copy(src, dst, copy_sems.at[len(local)])
        made.start()
        local.append(made)
        return made

    def at_block(b):
        return pl.ds(pl.multiple_of(b * block, block), block)

    def own_rows(b):
        return pl.ds(pl.multiple_of(b * block + g.s * half, half), half)

    down = Scatter(wires, w2, lambda i, j: own_w2.at[i, j], (rc, ry, None, None))
    half_at, do_at = wires.block(blocks), wires.block(blocks)
    first = [bring(cot, cot_v), bring(fc2, fc2_v), bring(slope, du_v), bring(fc1, fc1_v)]
    own = bring(w2.at[:, :, g.c], own_w2)
    later = [bring(n2, n2_v), bring(a, a_v), bring(h2, h2_v), bring(dense, dense_v)]
    later += [bring(heads.at[i, own_rows(b), :], heads_v.at[i, pl.ds(b * half, half)]) for i in range(seqs) for b in range(blocks)]
    enter(g)
    down.core_send()
    for made in first:
        made.wait()
    step = min(512, ff)
    per = step // ff_part

    def half_copy(b):
        return wires.copy(sent_v.at[b], got_v.at[b], half_at + b, half_at + b, 1 - g.s, g.k)

    def do_copy(b):
        return wires.copy(do_sent.at[b], do_v.at[b, g.s], do_at + b, do_at + b, 1 - g.s, g.k)

    small_v[...] = jnp.zeros_like(small_v)

    def split(b, total, keep, give):
        @pl.when(g.s == 0)
        def _():
            keep(total[:half])
            give[b] = total[half:].astype(bf16)

        @pl.when(g.s == 1)
        def _():
            keep(total[half:])
            give[b] = total[:half].astype(bf16)

    def du_step(b, sums):
        at = at_block(b)
        grad = cot_v[at, :]
        total, new = None, []
        for n in range(ff // step):
            cut = slice(n * step, (n + 1) * step)
            weight = fc2_v[n * per : (n + 1) * per].reshape(step, width)
            da = lax.dot_general(grad, weight, (((1,), (1,)), ((), ())), preferred_element_type=f32)
            du = (da * du_v[at, cut].astype(f32)).astype(bf16)
            du_v[at, cut] = du
            new.append(sums[n] + jnp.sum(du.astype(f32), axis=0, keepdims=True))
            weight = fc1_v[:, :, cut].reshape(width, step)
            term = lax.dot_general(du, weight, (((1,), (1,)), ((), ())), preferred_element_type=f32)
            total = term if total is None else total + term

        def keep(value):
            mine_v[b] = value

        split(b, total, keep, sent_v)

        @pl.when(b > 0)
        def _():
            half_copy(b - 1).start()

        @pl.when(b == 0)
        def _():
            own.wait()
            down.core_done()

        return tuple(new)

    zero = jnp.zeros((1, step), f32)
    sums = lax.fori_loop(0, blocks, du_step, (zero,) * (ff // step))
    for made in later:
        made.wait()

    @pl.loop(0, width // (4 * rows))
    def _(m):
        @pl.when(m == 0)
        def _():
            half_copy(blocks - 1).start()

        left = n2_v[:, pl.ds(pl.multiple_of(m * 4 * rows, 128), 4 * rows)]
        for n in range(ff // step):
            cut = slice(n * step, (n + 1) * step)
            out = lax.dot_general(left, du_v[:, cut], (((0,), (0,)), ((), ())), preferred_element_type=f32)
            w1_v[pl.ds(4 * m, 4), :, cut] = out.astype(bf16).reshape(4, rows, step)

    kept = [bring(w1_v, w1_out)]
    for n in range(ff // step):
        for i in range(per):
            small_v[n * per + i, 6:7, pl.ds(pl.multiple_of(g.s * ff_part, 128), ff_part)] = sums[n][
                :, i * ff_part : (i + 1) * ff_part
            ]

    def norm_step(b, sums):
        gains, biases, branch, cots = sums
        wires.arrived(got_v.at[b], half_at + b)
        grad = mine_v[b] + got_v[b].astype(f32)
        xhat, root = normalize(h2_v[b])
        gains = gains + jnp.sum(grad * xhat, axis=0, keepdims=True)
        biases = biases + jnp.sum(grad, axis=0, keepdims=True)
        cot_b = cot_v[own_rows(b), :].astype(f32)
        cots = cots + jnp.sum(cot_b, axis=0, keepdims=True)
        dh2 = cot_b + norm_pull(grad, vec[4:5, :width], xhat, root)
        mine_v[b] = dh2
        da = dh2.astype(bf16)
        branch = branch + jnp.sum(da.astype(f32), axis=0, keepdims=True)
        da_v[pl.ds(pl.multiple_of(b * half, half), half), :] = da
        grads = [
            lax.dot_general(
                da, dense_v[i * (shards // seqs) : (i + 1) * (shards // seqs)].reshape(part, width),
                (((1,), (1,)), ((), ())), preferred_element_type=f32,
            ).astype(bf16)
            for i in range(seqs)
        ]
        do_v[b, g.s] = jnp.where(g.s == 0, grads[0], grads[1])
        do_sent[b] = jnp.where(g.s == 0, grads[1], grads[0])

        @pl.when(b > 0)
        def _():
            do_copy(b - 1).start()

        return gains, biases, branch, cots

    zero = jnp.zeros((1, width), f32)
    sums = lax.fori_loop(0, blocks, norm_step, (zero,) * 4)
    kept.append(bring(mine_v, dh2_out))
    for row, vector in ((4, sums[0]), (5, sums[1]), (3, sums[2]), (7, sums[3])):
        for j in range(shards):
            small_v[j, row : row + 1, :rows] = vector[:, j * rows : (j + 1) * rows]
    do_copy(blocks - 1).start()
    kept.append(bring(small_v, small_out))

    for i in range(seqs):
        out = lax.dot_general(heads_v[i], da_v[...], (((0,), (0,)), ((), ())), preferred_element_type=f32).astype(bf16)
        wd_v[i * (shards // seqs) : (i + 1) * (shards // seqs)] = out.reshape(shards // seqs, rows, width)
    kept.append(bring(wd_v, wd_out))

    @pl.loop(0, blocks)
    def _(b):
        at = at_block(b)
        total = None
        for n in range(ff // step):
            weight = fc2_v[n * per : (n + 1) * per].reshape(step, width)
            term = jnp.dot(a_v[at, n * step : (n + 1) * step], weight, preferred_element_type=f32)
            total = term if total is None else total + term

        def keep(value):
            h2_v[b] = h2_v[b] + value + vec[7:8, :width]

        split(b, total, keep, got_v)

    kept += [bring(h2_v, keep_out), bring(got_v, give_out)]
    down.y_done()
    kept.append(bring(ry, ry_out))
    for b in range(blocks):
        wires.arrived(do_v.at[b, 1 - g.s], do_at + b)
    kept.append(bring(do_v, do_out))
    for b in range(blocks):
        half_copy(b).wait_send()
        do_copy(b).wait_send()
    wires.drain()
    for made in kept:
        made.wait()
    assert wires.used <= counts[0] and len(local) <= counts[1]


def middle_exchange(a, slope, n2, fc1, fc2, dense, cot, h2, heads, w2, vec, seqs, shards):
    blocks, half, width = h2.shape
    tokens, ff = a.shape
    part = width // seqs
    rows, ff_part = width // shards, ff // shards
    counts = (32, 40)
    any_, vmem = pl.BlockSpec(memory_space=pl.ANY), pl.BlockSpec(memory_space=pltpu.VMEM)
    own32, own16 = ((blocks, half, width), f32), ((blocks, half, width), bf16)
    do, smalls = ((blocks, seqs, half, part), bf16), ((shards, 8, 256), f32)
    w1, wd, ry = ((shards, rows, ff), bf16), ((shards, rows, width), bf16), ((4, ff_part, width), bf16)
    outs = [own32, do, w1, wd, own32, own16, ry, smalls]
    rc = ((4, 2, ff_part, width), bf16)
    scratch = [(v.shape, bf16) for v in (a, slope, n2, fc1, fc2, dense, cot)] + [
        own32, ((seqs, blocks * half, part), bf16), rc, w1, wd, own32, own16, own16, ((blocks * half, width), bf16), do,
        ((blocks, half, part), bf16), smalls, rc, ry,
    ]
    return pl.pallas_call(
        functools.partial(middle_kernel, seqs, shards, counts),
        in_specs=[any_] * 10 + [vmem],
        out_specs=[any_] * len(outs),
        out_shape=[jax.ShapeDtypeStruct(s, d) for s, d in outs],
        scratch_shapes=[pltpu.VMEM(s, d) for s, d in scratch]
        + [pltpu.SemaphoreType.DMA((counts[0],)), pltpu.SemaphoreType.DMA((counts[0],)), pltpu.SemaphoreType.DMA((counts[1],))],
        compiler_params=pltpu.CompilerParams(collective_id=3, has_side_effects=True, vmem_limit_bytes=62 * 2**20),
        name="middle_exchange",
    )(a, slope, n2, fc1, fc2, dense, cot, h2, heads, w2.reshape((4, 2, 2) + w2.shape[1:]), vec)


def backward_kernel(
    seqs, shards, counts,
    qkv, do, n1, qkvw, x_all, dh2, keep, give, ry2, w1, wd, smalls, vec, slopes,
    ret_y, ret_x, o_qkv, o_dense, o_up, o_down, o_small,
    qkv_v, do_v, dqkv_v, n1_v, qkvw_v, x_v, dh2_v, dk_acc, dv_acc, bias_acc, mine_v, sent_v, got_v, dx_v, gq_v,
    small_v, small_got, small_fin, small_last, f_qkv, f_dense, f_up, f_down, keep_v, give_v, y_v, own_w1, own_wd, idc, idr,
    *rest,
):
    bufs, (send_sems, recv_sems, copy_sems) = rest[:-3], rest[-3:]
    g = Geometry(seqs, shards)
    wires = Wires(g, send_sems, recv_sems)
    pairs, tokens = do_v.shape[0], do_v.shape[1]
    part = pairs * 2 * HEAD
    width = n1_v.shape[1]
    lanes = seqs * shards
    block = ROWS * lanes
    blocks = tokens // block
    half = block // seqs
    tile = bias_acc.shape[2]
    local = []

    def bring(src, dst):
        made = pltpu.make_async_copy(src, dst, copy_sems.at[len(local)])
        made.start()
        local.append(made)
        return made

    def held(ref):
        return lambda i, j: ref.at[i, j]

    down = Scatter(wires, None, None, (None,) + bufs[0:3])
    up = Scatter(wires, w1, held(own_w1), bufs[3:7])
    dense = Scatter(wires, wd, held(own_wd), bufs[7:11])
    qkv_sum = Scatter(wires, gq_v, lambda i, j: gq_v.at[i, j, g.c], bufs[11:15])
    back_y = Back(wires, y_v, ret_y, 1)
    give_at = wires.block(1)
    back_x = Back(wires, dx_v, ret_x, blocks)
    half_at = wires.block(blocks)
    small_at = wires.block(shards + 1)

    ry_in = bring(ry2, down.ry)
    first = [bring(qkv, qkv_v)] + [bring(do.at[:, pl.ds(h * 2 * HEAD, 2 * HEAD)], do_v.at[h]) for h in range(pairs)]
    owns = [bring(a.at[:, :, g.c], b) for a, b in ((w1, own_w1), (wd, own_wd))] + [bring(keep, keep_v)]
    later = [
        bring(n1, n1_v), bring(qkvw, qkvw_v), bring(x_all.at[:, pl.ds(g.s * shards, shards)], x_v), bring(dh2, dh2_v),
        bring(smalls, small_v),
    ]
    enter(g)
    idc[...] = blocked_ids(idc.shape, 0, lanes)
    idr[...] = blocked_ids(idr.shape, 1, lanes)
    up.core_send()
    dense.core_send()
    ry_in.wait()
    down.z_send()
    wires.send(give, give_v, give_at, 1 - g.s, g.k, give)
    for made in first + owns:
        made.wait()

    lane_id = lax.broadcasted_iota(jnp.int32, (1, 2 * HEAD), 1)

    def attend(h):
        q_ref, k_ref, v_ref, do_ref = qkv_v.at[h], qkv_v.at[pairs + h], qkv_v.at[2 * pairs + h], do_v.at[h]
        dk_acc[...] = jnp.zeros_like(dk_acc)
        dv_acc[...] = jnp.zeros_like(dv_acc)
        for j in range(2):
            bias_acc[j] = jnp.broadcast_to(slopes[g.s * pairs + h, j] * idc[...], bias_acc.shape[1:])
        cols = pl.ds(pl.multiple_of(h * 2 * HEAD, 2 * HEAD), 2 * HEAD)
        for b in range(blocks):
            end = (b + 1) * block
            for t in range(block // tile):
                at = pl.ds(b * block + t * tile, tile)
                q = q_ref[at, :] * jnp.asarray(HEAD**-0.5, bf16)
                grad = do_ref[at, :]
                ids_q = idr[:, at]
                both = None
                for j in range(2):
                    mine = (lane_id // HEAD) == j
                    qj = jnp.where(mine, q, jnp.zeros_like(q))
                    doj = jnp.where(mine, grad, jnp.zeros_like(grad))
                    s = lax.dot_general(
                        k_ref[:end, :], qj, (((1,), (1,)), ((), ())), preferred_element_type=f32
                    )
                    s = s + bias_acc[j, :end, :]
                    tail = attn_mask(s[b * block :, :], idc[b * block : end, :] <= ids_q)
                    s = jnp.concatenate([s[: b * block, :], tail], axis=0) if b else tail
                    top = jnp.max(s, axis=0, keepdims=True)
                    e = jnp.exp(s - top)
                    probs = e * (1.0 / jnp.sum(e, axis=0, keepdims=True))
                    dv_acc[:end, :] += jnp.dot(probs.astype(bf16), doj, preferred_element_type=f32)
                    dp = lax.dot_general(
                        v_ref[:end, :], doj, (((1,), (1,)), ((), ())), preferred_element_type=f32
                    )
                    inner = jnp.sum(probs * dp, axis=0, keepdims=True)
                    ds = (probs * (dp - inner)).astype(bf16)
                    dk_acc[:end, :] += jnp.dot(ds, qj, preferred_element_type=f32)
                    dq = lax.dot_general(
                        ds, k_ref[:end, :], (((0,), (0,)), ((), ())), preferred_element_type=f32
                    )
                    both = dq if both is None else jnp.where(mine, dq, both)
                dqkv_v[0, at, cols] = (both * (HEAD**-0.5)).astype(bf16)
        dqkv_v[1, :, cols] = dk_acc[...].astype(bf16)
        dqkv_v[2, :, cols] = dv_acc[...].astype(bf16)

    @pl.loop(0, pairs)
    def _(h):
        attend(h)

        @pl.when(h == 0)
        def _():
            up.core_done()

        @pl.when(h == 1)
        def _():
            dense.core_done()

        @pl.when(h == 2)
        def _():
            down.z_done()
            wires.arrived(give_v, give_at)

            @pl.loop(0, blocks)
            def _(b):
                y_v[b] = (keep_v[b] + give_v[b].astype(f32)).reshape(shards, ROWS, width).astype(bf16)

            back_y.send(0)

    for made in later:
        made.wait()

    rows = width // shards

    @pl.loop(0, blocks)
    def _(m):
        cut = n1_v[:, pl.ds(pl.multiple_of(m * block, block), block)]
        for p in range(3):
            out = lax.dot_general(cut, dqkv_v[p], (((0,), (0,)), ((), ())), preferred_element_type=f32).astype(bf16)
            out = out.reshape(block // rows // 2, 2, rows, part)
            for i in range(block // rows // 2):
                at = m * (block // rows // 2) + i
                for j in range(2):
                    gq_v[at // 2, at % 2, j, :, p * part : (p + 1) * part] = out[i, j]

    qkv_sum.core_send()

    def half_copy(b):
        return wires.copy(sent_v.at[b], got_v.at[b], half_at + b, half_at + b, 1 - g.s, g.k)

    @pl.loop(0, blocks)
    def _(b):
        total = None
        for p in range(3):
            weight = qkvw_v[:, :, p * part : (p + 1) * part].reshape(width, part)
            term = lax.dot_general(
                dqkv_v[p, pl.ds(pl.multiple_of(b * block, block), block), :], weight, (((1,), (1,)), ((), ())),
                preferred_element_type=f32,
            )
            total = term if total is None else total + term

        @pl.when(g.s == 0)
        def _():
            mine_v[b] = total[:half]
            sent_v[b] = total[half:].astype(bf16)

        @pl.when(g.s == 1)
        def _():
            mine_v[b] = total[half:]
            sent_v[b] = total[:half].astype(bf16)

        @pl.when(b == 2)
        def _():
            up.y_done()
            up.z_send()

        @pl.when(b > 0)
        def _():
            half_copy(b - 1).start()

    own_y = bring(y_v.at[:, g.k], ret_y.at[g.k])
    half_copy(blocks - 1).start()

    sums = [jnp.sum(dqkv_v[p].astype(f32), axis=0, keepdims=True) for p in (0, 2)]
    per = 2 * width // shards
    for i in range(part // per):
        for half_no in range(2):
            small_v[(half_no * width + g.s * part) // per + i, 2:3, :per] = sums[half_no][:, i * per : (i + 1) * per]
    qkv_sum.core_done()
    dense.y_done()
    dense.z_send()

    def norm_step(b, sums):
        wires.arrived(got_v.at[b], half_at + b)
        grad = mine_v[b] + got_v[b].astype(f32)
        xhat, root = normalize(x_v[b].astype(f32).reshape(half, width))
        gains = sums[0] + jnp.sum(grad * xhat, axis=0, keepdims=True)
        biases = sums[1] + jnp.sum(grad, axis=0, keepdims=True)
        dx = dh2_v[b] + norm_pull(grad, vec[0:1, :width], xhat, root)
        dx_v[b] = dx.reshape(shards, ROWS, width).astype(bf16)
        back_x.send(b)

        @pl.when(b == 0)
        def _():
            up.z_done()

        @pl.when(b == 2)
        def _():
            qkv_sum.y_done()
            qkv_sum.z_send()

        return gains, biases

    gains, biases = lax.fori_loop(0, blocks, norm_step, (jnp.zeros((1, width), f32),) * 2)
    for j in range(shards):
        small_v[j, 0:1, :rows] = gains[:, j * rows : (j + 1) * rows]
        small_v[j, 1:2, :rows] = biases[:, j * rows : (j + 1) * rows]
    kept = [own_y, bring(dx_v.at[:, g.k], ret_x.at[g.k])]
    for d in range(1, shards):
        to = (g.k + d) % shards
        wires.send(small_v.at[to], small_got.at[g.k], small_at + d, g.s, to, small_v.at[0])
    small_got[g.k] = small_v[g.k]
    down.final()
    dense.z_done()
    up.final()
    qkv_sum.z_done()
    for d in range(1, shards):
        wires.arrived(small_got.at[(g.k - d) % shards], small_at + d)
    small_fin[0] = jnp.sum(small_got[...], axis=0)
    wires.send(small_fin.at[0], small_fin.at[1], small_at + shards, 1 - g.s, g.k, small_fin.at[0])
    dense.final()

    down.done()
    ff_part = f_down.shape[0] // seqs
    for i, at in ((0, g.s), (1, 1 - g.s)):
        f_down[pl.ds(pl.multiple_of(at * ff_part, ff_part), ff_part), :] = down.fin[i].astype(f32)
    kept.append(bring(f_down, o_down))
    up.done()
    for i, at in ((0, g.s), (1, 1 - g.s)):
        for j in range(shards):
            f_up[:, pl.ds(pl.multiple_of((j * seqs + at) * ff_part, 128), ff_part)] = up.fin[
                i, :, j * ff_part : (j + 1) * ff_part
            ].astype(f32)
    kept.append(bring(f_up, o_up))
    dense.done()
    f_dense[...] = dense.fin[0].astype(f32) + dense.fin[1].astype(f32)
    kept.append(bring(f_dense, o_dense))
    wires.arrived(small_fin.at[1], small_at + shards)
    small_last[...] = small_fin[0] + small_fin[1]
    kept.append(bring(small_last, o_small))
    qkv_sum.final()
    qkv_sum.done()
    for i, at in ((0, g.s), (1, 1 - g.s)):
        for p in range(3):
            f_qkv[:, pl.ds(pl.multiple_of(p * width + at * part, 128), part)] = qkv_sum.fin[
                i, :, p * part : (p + 1) * part
            ].astype(f32)
    kept.append(bring(f_qkv, o_qkv))
    back_y.finish()
    back_x.finish()
    for b in range(blocks):
        half_copy(b).wait_send()
    wires.drain()
    for made in kept:
        made.wait()
    assert wires.used <= counts[0] and len(local) <= counts[1]


def backward_exchange(
    qkv, do, n1, qkvw, x_all, dh2, keep, give, ry2, w1, wd, smalls, vec, slopes, seqs, shards
):
    tokens, part = do.shape
    width = n1.shape[1]
    pairs = part // (2 * HEAD)
    lanes = seqs * shards
    block = ROWS * lanes
    blocks, half = tokens // block, block // seqs
    tile = min(256, block)
    rows, ff = width // shards, w1.shape[2]
    ff_part = ff // shards
    counts = (256, 48)
    cut = lambda a: a.reshape((4, 2, 2) + a.shape[1:])
    any_, vmem = pl.BlockSpec(memory_space=pl.ANY), pl.BlockSpec(memory_space=pltpu.VMEM)
    ret = (shards, blocks, ROWS, width)
    outs = [
        (ret, bf16), (ret, bf16), ((rows, 3 * width), f32), ((rows, width), f32), ((rows, seqs * ff), f32),
        ((seqs * ff_part, width), f32), (smalls.shape[1:], f32),
    ]
    blks = [(ff_part, width), (rows, ff), (rows, width), (rows, 3 * part)]
    scratch = [
        ((3 * pairs, tokens, 2 * HEAD), bf16), ((pairs, tokens, 2 * HEAD), bf16), ((3, tokens, part), bf16),
        ((tokens, width), bf16), ((shards, rows, 3 * part), bf16), ((blocks, shards, ROWS, width), bf16),
        ((blocks, half, width), f32), ((tokens, 2 * HEAD), f32), ((tokens, 2 * HEAD), f32), ((2, tokens, tile), f32),
        ((blocks, half, width), f32), ((blocks, half, width), bf16), ((blocks, half, width), bf16),
        ((blocks, shards, ROWS, width), bf16), ((4, 2, 2) + blks[3], bf16), (smalls.shape, f32), (smalls.shape, f32),
        ((2,) + smalls.shape[1:], f32), (smalls.shape[1:], f32), ((rows, 3 * width), f32), ((rows, width), f32), ((rows, seqs * ff), f32),
        ((seqs * ff_part, width), f32), ((blocks, half, width), f32), ((blocks, half, width), bf16),
        ((blocks, shards, ROWS, width), bf16), ((4, 2) + blks[1], bf16), ((4, 2) + blks[2], bf16),
        ((tokens, 1), f32), ((1, tokens), f32),
    ]
    for blk in blks:
        scratch += [((4, 2) + blk, bf16)] * (blk is not blks[0])
        scratch += [((4,) + blk, bf16), ((4,) + blk, bf16), ((2,) + blk, bf16)]
    return pl.pallas_call(
        functools.partial(backward_kernel, seqs, shards, counts),
        in_specs=[any_] * 12 + [vmem, pl.BlockSpec(memory_space=pltpu.SMEM)],
        out_specs=[any_] * len(outs),
        out_shape=[jax.ShapeDtypeStruct(s, d) for s, d in outs],
        scratch_shapes=[pltpu.VMEM(s, d) for s, d in scratch]
        + [pltpu.SemaphoreType.DMA((counts[0],)), pltpu.SemaphoreType.DMA((counts[0],)), pltpu.SemaphoreType.DMA((counts[1],))],
        compiler_params=pltpu.CompilerParams(collective_id=2, has_side_effects=True, vmem_limit_bytes=60 * 2**20),
        name="backward_exchange",
    )(
        qkv, do, n1, qkvw, x_all, dh2, keep, give, ry2, cut(w1), cut(wd), smalls, vec, slopes,
    )


def layout_tables(lengths, lane_count, group_count, per_group):
    seq_rows = lengths // lane_count
    row_start = jnp.cumsum(seq_rows) - seq_rows
    slot_rows = seq_rows.reshape(group_count, per_group)
    slot_start = row_start.reshape(group_count, per_group)
    slot_before = jnp.cumsum(slot_rows, axis=1) - slot_rows
    return seq_rows, row_start, slot_rows, slot_start, slot_before


def per_device(
    tokens, cotangent, lengths, first_gain, first_bias, qkv_weight, qv_bias, dense_weight, dense_bias,
    second_gain, second_bias, fc1_weight, fc1_bias, fc2_weight, fc2_bias,
):
    shards, seqs = lax.axis_size("shard"), lax.axis_size("seq")
    lanes = shards * seqs
    slots, width = tokens.shape[1], tokens.shape[2]
    rows = slots // shards
    blocks = rows // ROWS

    smalls_in = (first_gain, first_bias, qv_bias, dense_bias, second_gain, second_bias, fc1_bias, fc2_bias)
    small = jnp.stack([jnp.pad(a.astype(f32), (0, 256 - a.shape[0])) for a in smalls_in])
    slopes = jnp.asarray(np.exp2(-8.0 * (np.arange(HEADS) + 1.0) / HEADS).reshape(-1, 2), f32)

    seq_rows = lengths // lanes
    number = jnp.arange(shards, dtype=jnp.int32)
    row_start = jnp.sum(jnp.where(number[None, :] < number[:, None], seq_rows[None, :], 0), axis=1)
    window = (row_start[:, None] + jnp.arange(rows, dtype=jnp.int32)[None, :]).reshape(-1)

    def pack(source):
        return jnp.take(source, window, axis=0, mode="clip").reshape(shards, blocks, ROWS, width)

    (
        x_all, cot_all, normed_one, normed_two, full_qkv, full_dense, full_up, full_down, qkv, mixed, resid, activ, slope,
        grad_down, vectors,
    ) = forward_exchange(
        pack(tokens[0]), pack(cotangent[0]), qkv_weight, small, dense_weight, fc1_weight, fc2_weight,
        slopes, lengths, seqs, shards,
    )
    grad_resid, grad_mixed, grad_up, grad_dense, keep, give, half_sums, small_grads = middle_exchange(
        activ, slope, normed_two, full_up, full_down, full_dense, cot_all, resid, mixed, grad_down, vectors, seqs, shards
    )
    ret_out, ret_grad, g_qkv, g_dense, g_up, g_down, g_small = backward_exchange(
        qkv, grad_mixed.reshape(slots * seqs, width // seqs), normed_one, full_qkv, x_all, grad_resid, keep, give, half_sums,
        grad_up, grad_dense, small_grads, vectors, slopes, seqs, shards,
    )

    row_here = jnp.arange(slots, dtype=jnp.int32)[:, None]
    inside = (row_here >= row_start[None]) & (row_here < (row_start + seq_rows)[None])
    fetch = jnp.sum(jnp.where(inside, number[None] * rows + row_here - row_start[None], 0), axis=1)
    fetch_live = jnp.arange(slots, dtype=jnp.int32) < jnp.sum(seq_rows)

    def to_stream(got):
        taken = jnp.take(got.reshape(-1, width), fetch, axis=0, mode="clip")
        return jnp.where(fetch_live[:, None], taken, jnp.zeros_like(taken))[None]

    vectors_out = tuple(g_small[i, : a.shape[0]] for i, a in enumerate(smalls_in))
    g_gain_one, g_bias_one, g_qv, g_bdense, g_gain_two, g_bias_two, g_bup, g_bdown = vectors_out
    return (
        to_stream(ret_out), to_stream(ret_grad),
        g_gain_one, g_bias_one, g_qkv, g_qv, g_dense, g_bdense, g_gain_two, g_bias_two, g_up, g_bup, g_down, g_bdown,
    )


def per_device_any(
    tokens, cotangent, lengths, first_gain, first_bias, qkv_weight, qv_bias, dense_weight, dense_bias,
    second_gain, second_bias, fc1_weight, fc1_bias, fc2_weight, fc2_bias,
):
    shards, seqs = lax.axis_size("shard"), lax.axis_size("seq")
    lanes = shards * seqs
    slots, width = tokens.shape[1], tokens.shape[2]
    rows = slots // shards
    cap = slots * seqs
    per_group = lengths.shape[0] // shards
    hidden_units = fc1_weight.shape[1]
    me, group = lax.axis_index("seq"), lax.axis_index("shard")
    blocks = rows // ROWS
    heads = width // HEAD // seqs
    part = heads * HEAD
    ff_part = hidden_units // shards // seqs

    qkv_half = take(qkv_weight.reshape(-1, 3, seqs, part), me, 2).reshape(-1, 3 * part)
    fc1_half = take(fc1_weight.reshape(-1, shards, seqs, ff_part), me, 2).reshape(-1, shards * ff_part)
    fc2_half = take(fc2_weight.reshape(seqs, ff_part, width), me, 0)
    small = jnp.concatenate(
        [first_gain, first_bias, qv_bias, dense_bias, second_gain, second_bias, fc1_bias, fc2_bias]
    )
    small_rows = -(-small.shape[0] // (3 * part))
    small_rows += -small_rows % 16
    small = jnp.pad(small, (0, small_rows * 3 * part - small.shape[0])).reshape(small_rows, 3 * part)
    gather = lambda a: lax.all_gather(a, "shard", axis=0, tiled=False)
    qkv_small = gather(jnp.concatenate([qkv_half, small], axis=0))
    own_rows = qkv_half.shape[0]
    full_qkv = qkv_small[:, :own_rows].reshape(width, 3 * part)
    smalls = qkv_small[:, own_rows:].reshape(shards, -1).astype(f32)
    full_dense = gather(dense_weight).reshape(width, width)
    full_up = gather(fc1_half).reshape(width, shards * ff_part)
    full_down = gather(fc2_half).reshape(shards * ff_part, width)
    cuts, at = [], 0
    for a in (first_gain, first_bias, qv_bias, dense_bias, second_gain, second_bias, fc1_bias, fc2_bias):
        cuts.append(smalls[:, at : at + a.shape[0]].reshape(-1))
        at += a.shape[0]
    gain_one, bias_one, bias_qv, bias_dense, gain_two, bias_two, bias_up, bias_down = cuts
    bias_q, bias_v = (take(bias_qv[i * width : (i + 1) * width].reshape(seqs, part), me) for i in (0, 1))
    bias_all = jnp.concatenate([bias_q, jnp.zeros_like(bias_q), bias_v])
    bias_up = take(bias_up.reshape(shards, seqs, ff_part), me, 1).reshape(-1)

    seq_rows, row_start, slot_rows, slot_start, slot_before = layout_tables(lengths, lanes, shards, per_group)
    row_in = jnp.arange(rows, dtype=jnp.int32)[None, :, None]
    inside = ((row_in >= slot_before[:, None]) & (row_in < (slot_before + slot_rows)[:, None])).astype(jnp.int32)
    send_live = jnp.sum(inside, axis=2) > 0
    send_row = jnp.sum(inside * (slot_start[:, None] + row_in - slot_before[:, None]), axis=2).reshape(-1)

    def to_groups(source):
        packed = jnp.take(source, send_row, axis=0).reshape(shards, rows, width)
        packed = jnp.where(send_live[:, :, None], packed, jnp.zeros_like(packed))
        got = lax.all_to_all(packed, "shard", split_axis=0, concat_axis=0, tiled=True)
        own = got.reshape(shards, blocks, ROWS, width).transpose(1, 0, 2, 3).reshape(blocks, -1, width)
        return own, seq_gather(own, 1).reshape(cap, width)

    x_own, x_low = to_groups(tokens[0])
    cot_own, cot_low = to_groups(cotangent[0])

    def own_part(whole):
        return take(whole.reshape(blocks, seqs, -1, whole.shape[-1]), me, 1)

    place = jnp.arange(cap, dtype=jnp.int32)
    block_of, in_block = place // (ROWS * lanes), place % (ROWS * lanes)
    row_of = block_of * ROWS + in_block % ROWS
    ids = row_of * lanes + in_block // ROWS
    own_before, own_count = take(slot_before, group), take(slot_rows, group)
    holds = (row_of[:, None] >= own_before[None]) & (row_of[:, None] < (own_before + own_count)[None])
    begin_row = jnp.sum(jnp.where(holds, own_before[None], 0), axis=1)
    begins = jnp.where(jnp.any(holds, axis=1), begin_row * lanes, ids)
    ids, begins = ids.astype(f32), begins.astype(f32)
    head_ids = me * heads + jnp.arange(heads, dtype=jnp.int32)
    slopes = 2.0 ** (-8.0 * (head_ids.astype(f32) + 1.0) / HEADS)
    one_seq = per_group == 1

    hidden = x_low.astype(f32)
    xhat_one, _ = normalize(hidden)
    normed_one = (xhat_one * gain_one + bias_one).astype(bf16)
    qkv = (jnp.dot(normed_one, full_qkv, preferred_element_type=f32) + bias_all).astype(bf16)
    mixed = attention_forward(qkv, slopes, ids, begins, lanes, one_seq)
    mixed_all = seq_gather(mixed, 1).reshape(cap, width)
    branch = jnp.dot(mixed_all, full_dense, preferred_element_type=f32) + bias_dense
    resid = hidden + branch
    xhat_two, _ = normalize(resid)
    normed_two = (xhat_two * gain_two + bias_two).astype(bf16)
    upper = jnp.dot(normed_two, full_up, preferred_element_type=f32) + bias_up
    activ = gelu_tanh(upper).astype(bf16)
    down = jnp.dot(activ, full_down, preferred_element_type=f32)
    resid_own = own_part(resid)
    down_own = seq_sum(down.reshape(blocks, seqs, -1, width), 1)
    block_out = (resid_own + down_own + bias_down).astype(bf16)

    grad_down = jnp.dot(activ.T, cot_low, preferred_element_type=f32).astype(bf16)
    grad_activ = jnp.dot(cot_low, full_down.T, preferred_element_type=f32)
    grad_upper = jax.vjp(gelu_tanh, upper)[1](grad_activ)[0].astype(bf16)
    grad_up = jnp.dot(normed_two.T, grad_upper, preferred_element_type=f32).astype(bf16)
    grad_bup = jnp.sum(grad_upper.astype(f32), axis=0)
    grad_normed = jnp.dot(grad_upper, full_up.T, preferred_element_type=f32)
    grad_normed = seq_sum(grad_normed.reshape(blocks, seqs, -1, width), 1).reshape(slots, width)
    cot_full = cot_own.reshape(slots, width).astype(f32)
    grad_bdown = jnp.sum(cot_full, axis=0)
    xhat_two, root_two = normalize(resid_own.reshape(slots, width))
    grad_gain_two = jnp.sum(grad_normed * xhat_two, axis=0)
    grad_bias_two = jnp.sum(grad_normed, axis=0)
    grad_resid = cot_full + norm_pull(grad_normed, gain_two, xhat_two, root_two)

    grad_branch = grad_resid.astype(bf16)
    grad_dense = jnp.dot(own_part(mixed_all).reshape(slots, width).T, grad_branch, preferred_element_type=f32).astype(bf16)
    grad_bdense = jnp.sum(grad_branch.astype(f32), axis=0)
    grad_mixed = jnp.dot(grad_branch, full_dense.T, preferred_element_type=f32).astype(bf16)
    got = seq_blocks(grad_mixed.reshape(blocks, -1, seqs, part), 2, bf16)
    if seqs == 2:
        grad_mixed = jnp.where(me == 0, jnp.stack(got, 1), jnp.stack(got[::-1], 1))
    else:
        grad_mixed = jnp.zeros((blocks, seqs) + got[0].shape[1:], bf16)
        for d, g in enumerate(got):
            grad_mixed = lax.dynamic_update_index_in_dim(grad_mixed, g, (me - d) % seqs, 1)
    grad_mixed = grad_mixed.reshape(cap, part)
    planes = qkv.reshape(cap, -1, 2 * HEAD).transpose(1, 0, 2)
    grad_proj = jnp.concatenate(
        attention_backward(planes, grad_mixed, slopes, ids, begins, lanes, one_seq), axis=1
    )
    grad_qkv = jnp.dot(normed_one.T, grad_proj, preferred_element_type=f32).astype(bf16)
    proj_sums = jnp.sum(grad_proj.astype(f32), axis=0)
    grad_one = jnp.dot(grad_proj, full_qkv.T, preferred_element_type=f32)
    grad_one = seq_sum(grad_one.reshape(blocks, seqs, -1, width), 1).reshape(slots, width)
    xhat_one, root_one = normalize(x_own.reshape(slots, width).astype(f32))
    grad_gain_one = jnp.sum(grad_one * xhat_one, axis=0)
    grad_bias_one = jnp.sum(grad_one, axis=0)
    tokens_grad = (grad_resid + norm_pull(grad_one, gain_one, xhat_one, root_one)).astype(bf16)

    row_here = jnp.arange(slots, dtype=jnp.int32)[:, None]
    seq_in = ((row_here >= row_start[None]) & (row_here < (row_start + seq_rows)[None])).astype(jnp.int32)
    home = jnp.arange(lengths.shape[0], dtype=jnp.int32) // per_group
    fetch = jnp.sum(seq_in * (home[None] * rows + slot_before.reshape(-1)[None] + row_here - row_start[None]), axis=1)
    fetch_live = jnp.sum(seq_in, axis=1) > 0

    def to_stream(own):
        sent = own.reshape(blocks, shards, ROWS, width).transpose(1, 0, 2, 3).reshape(shards, rows, width)
        got = lax.all_to_all(sent, "shard", split_axis=0, concat_axis=0, tiled=True)
        taken = jnp.take(got.reshape(-1, width), fetch, axis=0)
        return jnp.where(fetch_live[:, None], taken, jnp.zeros_like(taken))[None]

    down_block = shard_reduce(grad_down.reshape(shards, ff_part, width), bf16)
    up_block = shard_reduce(grad_up.reshape(shards, -1, shards * ff_part), bf16)
    dense_block = shard_reduce(grad_dense.reshape(shards, -1, width), bf16)
    qkv_block = shard_reduce(grad_qkv.reshape(shards, -1, 3 * part), bf16)

    def spread(vector, index_shape):
        zero = jnp.zeros(index_shape, f32)
        return lax.dynamic_update_index_in_dim(zero, vector, me, 1)

    sums = proj_sums.reshape(3, part)
    qv = spread(jnp.stack([sums[0], sums[2]]), (2, seqs, part)).reshape(shards, -1)
    bup = spread(grad_bup.reshape(shards, ff_part), (shards, seqs, ff_part)).reshape(shards, -1)
    rest = (grad_gain_one, grad_bias_one, grad_bdense, grad_gain_two, grad_bias_two, grad_bdown)
    packed = jnp.concatenate([a.reshape(shards, -1) for a in rest] + [qv, bup], axis=1)
    packed = shard_reduce(packed, f32)
    packed = jnp.sum(seq_gather(packed, 0), axis=0)
    cuts, at = [], 0
    for a in [a.reshape(shards, -1) for a in rest] + [qv, bup]:
        cuts.append(packed[at : at + a.shape[1]])
        at += a.shape[1]
    g_gain_one, g_bias_one, g_bdense, g_gain_two, g_bias_two, g_bdown, g_qv, g_bup = cuts

    g_dense = jnp.sum(seq_gather(dense_block.astype(bf16), 0).astype(f32), axis=0)
    g_qkv = seq_gather(qkv_block.astype(bf16).reshape(-1, 3, part), 2).reshape(-1, 3 * width).astype(f32)
    g_up = seq_gather(up_block.astype(bf16).reshape(-1, shards, ff_part), 2).reshape(-1, hidden_units).astype(f32)
    g_down = seq_gather(down_block.astype(bf16), 0).reshape(-1, width).astype(f32)
    return (
        to_stream(block_out), to_stream(tokens_grad.reshape(blocks, -1, width)),
        g_gain_one, g_bias_one, g_qkv, g_qv, g_dense, g_bdense, g_gain_two, g_bias_two, g_up, g_bup, g_down, g_bdown,
    )


def choose(*arguments):
    one = arguments[2].shape[0] == lax.axis_size("shard")
    fused = one and lax.axis_size("seq") == 2 and shard_factors(lax.axis_size("shard")) == (4, 2, 2)
    return (per_device if fused else per_device_any)(*arguments)


def solution(mesh):
    rows, vector, stream = P("shard", None), P("shard"), P(("seq", "shard"), None, None)
    params = (vector, vector, rows, vector, rows, vector, vector, vector, rows, vector, rows, vector)
    return jax.shard_map(
        choose, mesh=mesh, in_specs=(stream, stream, P()) + params, out_specs=(stream, stream) + params, check_vma=False
    )
```

profile of v0, /device:TPU:0, one launch (start us, length us, event | category | flops | bytes accessed | tf_op | source)
XLA Modules:
  0.0 343.6 jit_solution(5025276282088815414)
XLA Ops:
  0.6 0.0 copy-start
  0.7 1.4 fusion.1
  2.0 0.1 select_reduce_fusion.1
  2.2 0.1 iota_add_fusion
  2.2 0.1 reshape.151
  2.3 0.0 copy-start.2
  2.3 2.8 gather_fusion
  5.2 2.8 gather_fusion.1
  8.3 0.6 stack.46.small
  8.9 147.4 %forward_exchange.1 = (bf16[4,32,8,1024]{3,2,1,0:T(8,128)(2,1)}, bf16[1024,1024]{1,0:T(8,128)(2,1)}, bf16[1024,1024]{1,0:T(8,128)(2,1)}, bf16[1024,1024]{1,0:T(8...) custom-call(bf16[16,4,8,1024]{3,2,1,0:T(8,128)(2,1)} %bitcast.35, ...), custom_call_target="tpu_custom_call" | custom-call | tf_op jit(solution)/shard_map/forward_exchange/pallas_call | solution.py:732
  156.3 49.5 %middle_exchange.1 = (f32[4,128,1024]{2,1,0:T(8,128)}, bf16[4,2,128,512]{3,2,1,0:T(8,128)(2,1)}, bf16[16,64,2048]{2,1,0:T(8,128)(2,1)}, bf16[16,64,1024]{2,1,0:T...) custom-call(bf16[1024,2048]{1,0:T(8,128)(2,1)} %get-tuple-element.45, ...), custom_call_target="tpu_custom_call" | custom-call | tf_op jit(solution)/shard_map/middle_exchange/pallas_call | solution.py:1041
  205.8 124.0 %backward_exchange.1 = (bf16[16,4,8,1024]{3,2,1,0:T(8,128)(2,1)}, bf16[16,4,8,1024]{3,2,1,0:T(8,128)(2,1)}, f32[64,3072]{1,0:T(8,128)}, f32[64,1024]{1,0:T(8,128...) custom-call(bf16[12,1024,128]{2,1,0:T(8,128)(2,1)} %get-tuple-element.44.qkv, ...), custom_call_target="tpu_custom_call" | custom-call | tf_op jit(solution)/shard_map/backward_exchange/pallas_call | solution.py:1353
  329.8 0.1 select_reduce_fusion
  329.9 4.2 %gather_fusion.2 = bf16[512,1024]{1,0:T(8,128)(2,1)S(1)} fusion(bf16[512,1024]{1,0:T(8,128)(2,1)} %bitcast.32, s32[1024]{0:T(1024)S(1)} %pad_clamp_fusion), kind=kCustom, calls=%fused_computation.2 | custom fusion | bytes 2099200 | tf_op jit(solution)/shard_map/jit(_take)/gather | solution.py:1419
  334.1 2.1 gather_fusion.3
  336.2 0.7 iota_compare_fusion.3
  336.9 1.5 bitcast_select_fusion
  338.4 0.5 slice_bitcast_fusion
  338.9 0.6 slice.30
  339.5 0.5 slice_bitcast_fusion.4
  340.0 0.9 copy.34
  340.9 0.7 copy.35
  341.6 1.0 copy.36
  342.6 1.0 copy.37
  (52 shorter events, 0.2 us)
Async XLA Ops:
  0.6 1.7 copy-start
  2.3 2.8 copy-start.2
  5.1 2.9 copy-start.9
  5.1 2.9 copy-start.10
  5.1 2.9 copy-start.11
  5.1 2.9 copy-start.12
  5.2 3.0 copy-start.13
  5.2 3.0 copy-start.14
  5.2 3.0 copy-start.15
  5.2 3.0 copy-start.16
  329.9 4.2 %copy-start.3 = (bf16[16,4,8,1024]{3,2,1,0:T(8,128)(2,1)S(1)}, bf16[16,4,8,1024]{3,2,1,0:T(8,128)(2,1)}, u32[]{:S(2)}) copy-start(bf16[16,4,8,1024]{3,2,1,0:T(8,128)(2,1)} %get-tuple-element.68) | copy-start | bytes 3145732
  336.9 1.6 copy-start.8
  336.9 3.2 copy-start.6
  336.9 4.0 %copy-start.7 = (f32[64,1024]{1,0:T(8,128)S(1)}, f32[64,1024]{1,0:T(8,128)}, u32[]{:S(2)}) copy-start(f32[64,1024]{1,0:T(8,128)} %get-tuple-element.104) | copy-start | bytes 786436
  338.4 3.2 copy-start.5
  340.0 2.6 copy-start.4
  340.9 2.7 copy-start.1
where the time goes:
time: 344 us
  Pallas kernels  321 us (93%)
  local copies, waits for them, and re-layouts  17.2 us (5%)
  other arithmetic  4.47 us (1%)
    pallas_call x1, Pallas kernels, forward_exchange(): pl.pallas_call(functools.partial(forward_kernel, seqs, shards, counts), i...  147 us
    pallas_call x1, Pallas kernels, backward_exchange(): pl.pallas_call(functools.partial(backward_kernel, seqs, shards, counts),...  124 us
    pallas_call x1, Pallas kernels, middle_exchange(): pl.pallas_call(functools.partial(middle_kernel, seqs, shards, counts), in...  49.5 us

commit v1 on v0

--- a/solution.py
+++ b/solution.py
@@ -764,6 +764,11 @@
         g = self.g
         self.w.arrived(self.rc, self.at)
         self.add(8, lambda i: self.rc.at[i // 2, i % 2], lambda i: self.own(i // 2, i % 2))
+        if self.ry is not None:
+            self.y_send()
+
+    def y_send(self):
+        g = self.g
         self.w.send(self.rc.at[:, 1 - g.y], self.ry, self.at + 1, g.s, g.slot(0, 1, 0), self.ry)
 
     def y_done(self):
@@ -835,9 +840,9 @@
 def middle_kernel(
     seqs, shards, counts,
     a, slope, n2, fc1, fc2, dense, cot, h2, heads, w2, vec,
-    dh2_out, do_out, w1_out, wd_out, keep_out, give_out, ry_out, small_out,
+    dh2_out, do_out, rc1_out, wd_out, keep_out, give_out, ry_out, small_out,
     a_v, du_v, n2_v, fc1_v, fc2_v, dense_v, cot_v, h2_v, heads_v, own_w2, w1_v, wd_v, mine_v, sent_v, got_v,
-    da_v, do_v, do_sent, small_v, rc, ry,
+    da_v, do_v, do_sent, small_v, rc, ry, rc1,
     send_sems, recv_sems, copy_sems,
 ):
     g = Geometry(seqs, shards)
@@ -863,6 +868,7 @@
         return pl.ds(pl.multiple_of(b * block + g.s * half, half), half)
 
     down = Scatter(wires, w2, lambda i, j: own_w2.at[i, j], (rc, ry, None, None))
+    up = Scatter(wires, w1_v, lambda i, j: w1_v.at[i, j, g.c], (rc1, None, None, None))
     half_at, do_at = wires.block(blocks), wires.block(blocks)
     first = [bring(cot, cot_v), bring(fc2, fc2_v), bring(slope, du_v), bring(fc1, fc1_v)]
     own = bring(w2.at[:, :, g.c], own_w2)
@@ -940,9 +946,10 @@
         for n in range(ff // step):
             cut = slice(n * step, (n + 1) * step)
             out = lax.dot_general(left, du_v[:, cut], (((0,), (0,)), ((), ())), preferred_element_type=f32)
-            w1_v[pl.ds(4 * m, 4), :, cut] = out.astype(bf16).reshape(4, rows, step)
-
-    kept = [bring(w1_v, w1_out)]
+            w1_v[m, :, :, :, cut] = out.astype(bf16).reshape(2, 2, rows, step)
+
+    up.core_send()
+    kept = []
     for n in range(ff // step):
         for i in range(per):
             small_v[n * per + i, 6:7, pl.ds(pl.multiple_of(g.s * ff_part, 128), ff_part)] = sums[n][
@@ -1008,6 +1015,8 @@
         split(b, total, keep, got_v)
 
     kept += [bring(h2_v, keep_out), bring(got_v, give_out)]
+    up.core_done()
+    kept.append(bring(rc1, rc1_out))
     down.y_done()
     kept.append(bring(ry, ry_out))
     for b in range(blocks):
@@ -1032,11 +1041,13 @@
     own32, own16 = ((blocks, half, width), f32), ((blocks, half, width), bf16)
     do, smalls = ((blocks, seqs, half, part), bf16), ((shards, 8, 256), f32)
     w1, wd, ry = ((shards, rows, ff), bf16), ((shards, rows, width), bf16), ((4, ff_part, width), bf16)
-    outs = [own32, do, w1, wd, own32, own16, ry, smalls]
+    w1 = ((4, 2, 2, rows, ff), bf16)
+    rc1 = ((4, 2, rows, ff), bf16)
+    outs = [own32, do, rc1, wd, own32, own16, ry, smalls]
     rc = ((4, 2, ff_part, width), bf16)
     scratch = [(v.shape, bf16) for v in (a, slope, n2, fc1, fc2, dense, cot)] + [
         own32, ((seqs, blocks * half, part), bf16), rc, w1, wd, own32, own16, own16, ((blocks * half, width), bf16), do,
-        ((blocks, half, part), bf16), smalls, rc, ry,
+        ((blocks, half, part), bf16), smalls, rc, ry, rc1,
     ]
     return pl.pallas_call(
         functools.partial(middle_kernel, seqs, shards, counts),
@@ -1052,10 +1063,10 @@
 
 def backward_kernel(
     seqs, shards, counts,
-    qkv, do, n1, qkvw, x_all, dh2, keep, give, ry2, w1, wd, smalls, vec, slopes,
+    qkv, do, n1, qkvw, x_all, dh2, keep, give, ry2, rc1, wd, smalls, vec, slopes,
     ret_y, ret_x, o_qkv, o_dense, o_up, o_down, o_small,
     qkv_v, do_v, dqkv_v, n1_v, qkvw_v, x_v, dh2_v, dk_acc, dv_acc, bias_acc, mine_v, sent_v, got_v, dx_v, gq_v,
-    small_v, small_got, small_fin, small_last, f_qkv, f_dense, f_up, f_down, keep_v, give_v, y_v, own_w1, own_wd, idc, idr,
+    small_v, small_got, small_fin, small_last, f_qkv, f_dense, f_up, f_down, keep_v, give_v, y_v, own_wd, idc, idr,
     *rest,
 ):
     bufs, (send_sems, recv_sems, copy_sems) = rest[:-3], rest[-3:]
@@ -1081,18 +1092,19 @@
         return lambda i, j: ref.at[i, j]
 
     down = Scatter(wires, None, None, (None,) + bufs[0:3])
-    up = Scatter(wires, w1, held(own_w1), bufs[3:7])
+    up = Scatter(wires, None, None, bufs[3:7])
     dense = Scatter(wires, wd, held(own_wd), bufs[7:11])
     qkv_sum = Scatter(wires, gq_v, lambda i, j: gq_v.at[i, j, g.c], bufs[11:15])
-    back_y = Back(wires, y_v, ret_y, 1)
-    give_at = wires.block(1)
+    back_y = Back(wires, y_v, ret_y, blocks)
+    give_at = wires.block(blocks)
     back_x = Back(wires, dx_v, ret_x, blocks)
     half_at = wires.block(blocks)
     small_at = wires.block(shards + 1)
 
+    rc_in = bring(rc1, up.rc)
     ry_in = bring(ry2, down.ry)
     first = [bring(qkv, qkv_v)] + [bring(do.at[:, pl.ds(h * 2 * HEAD, 2 * HEAD)], do_v.at[h]) for h in range(pairs)]
-    owns = [bring(a.at[:, :, g.c], b) for a, b in ((w1, own_w1), (wd, own_wd))] + [bring(keep, keep_v)]
+    owns = [bring(a.at[:, :, g.c], b) for a, b in ((wd, own_wd),)] + [bring(keep, keep_v)]
     later = [
         bring(n1, n1_v), bring(qkvw, qkvw_v), bring(x_all.at[:, pl.ds(g.s * shards, shards)], x_v), bring(dh2, dh2_v),
         bring(smalls, small_v),
@@ -1100,11 +1112,13 @@
     enter(g)
     idc[...] = blocked_ids(idc.shape, 0, lanes)
     idr[...] = blocked_ids(idr.shape, 1, lanes)
-    up.core_send()
+    rc_in.wait()
+    up.y_send()
     dense.core_send()
     ry_in.wait()
     down.z_send()
-    wires.send(give, give_v, give_at, 1 - g.s, g.k, give)
+    for b in range(blocks):
+        wires.send(give.at[b], give_v.at[b], give_at + b, 1 - g.s, g.k, give.at[b])
     for made in first + owns:
         made.wait()
 
@@ -1159,22 +1173,17 @@
 
         @pl.when(h == 0)
         def _():
-            up.core_done()
-
-        @pl.when(h == 1)
-        def _():
             dense.core_done()
 
         @pl.when(h == 2)
         def _():
             down.z_done()
-            wires.arrived(give_v, give_at)
-
-            @pl.loop(0, blocks)
-            def _(b):
-                y_v[b] = (keep_v[b] + give_v[b].astype(f32)).reshape(shards, ROWS, width).astype(bf16)
-
-            back_y.send(0)
+
+        @pl.loop(blocks * h // pairs, blocks * (h + 1) // pairs)
+        def _(b):
+            wires.arrived(give_v.at[b], give_at + b)
+            y_v[b] = (keep_v[b] + give_v[b].astype(f32)).reshape(shards, ROWS, width).astype(bf16)
+            back_y.send(b)
 
     for made in later:
         made.wait()
@@ -1316,7 +1325,7 @@
 
 
 def backward_exchange(
-    qkv, do, n1, qkvw, x_all, dh2, keep, give, ry2, w1, wd, smalls, vec, slopes, seqs, shards
+    qkv, do, n1, qkvw, x_all, dh2, keep, give, ry2, rc1, wd, smalls, vec, slopes, seqs, shards
 ):
     tokens, part = do.shape
     width = n1.shape[1]
@@ -1325,7 +1334,7 @@
     block = ROWS * lanes
     blocks, half = tokens // block, block // seqs
     tile = min(256, block)
-    rows, ff = width // shards, w1.shape[2]
+    rows, ff = width // shards, rc1.shape[3]
     ff_part = ff // shards
     counts = (256, 48)
     cut = lambda a: a.reshape((4, 2, 2) + a.shape[1:])
@@ -1344,7 +1353,7 @@
         ((blocks, shards, ROWS, width), bf16), ((4, 2, 2) + blks[3], bf16), (smalls.shape, f32), (smalls.shape, f32),
         ((2,) + smalls.shape[1:], f32), (smalls.shape[1:], f32), ((rows, 3 * width), f32), ((rows, width), f32), ((rows, seqs * ff), f32),
         ((seqs * ff_part, width), f32), ((blocks, half, width), f32), ((blocks, half, width), bf16),
-        ((blocks, shards, ROWS, width), bf16), ((4, 2) + blks[1], bf16), ((4, 2) + blks[2], bf16),
+        ((blocks, shards, ROWS, width), bf16), ((4, 2) + blks[2], bf16),
         ((tokens, 1), f32), ((1, tokens), f32),
     ]
     for blk in blks:
@@ -1360,7 +1369,7 @@
         compiler_params=pltpu.CompilerParams(collective_id=2, has_side_effects=True, vmem_limit_bytes=60 * 2**20),
         name="backward_exchange",
     )(
-        qkv, do, n1, qkvw, x_all, dh2, keep, give, ry2, cut(w1), cut(wd), smalls, vec, slopes,
+        qkv, do, n1, qkvw, x_all, dh2, keep, give, ry2, rc1, cut(wd), smalls, vec, slopes,
     )
 
 

time: 344 us -> 337 us (0.980)
  Pallas kernels: 321 us -> 314 us
    pallas_call x1, Pallas kernels: 124 us -> 117 us  [backward_exchange(): pl.pallas_call(functools.partial(backward_kernel, seqs, shards, counts),...]
where the time goes in v1:
time: 337 us; the launch traced here: 336 us
  Pallas kernels  314 us (93%)
  local copies, waits for them, and re-layouts  17.2 us (5%)
  other arithmetic  4.47 us (1%)
    pallas_call x1, Pallas kernels, forward_exchange(): pl.pallas_call(functools.partial(forward_kernel, seqs, shards, counts), i...  147 us
    pallas_call x1, Pallas kernels, backward_exchange(): pl.pallas_call(functools.partial(backward_kernel, seqs, shards, counts),...  117 us
    pallas_call x1, Pallas kernels, middle_exchange(): pl.pallas_call(functools.partial(middle_kernel, seqs, shards, counts), in...  49.5 us

profile of v1, /device:TPU:0, one launch (start us, length us, event | category | flops | bytes accessed | tf_op | source)
XLA Modules:
  0.0 336.4 jit_solution(732166266625500989)
XLA Ops:
  0.6 0.0 copy-start
  0.7 1.4 fusion.1
  2.0 0.1 select_reduce_fusion.1
  2.2 0.1 iota_add_fusion
  2.2 0.1 reshape.147
  2.3 0.0 copy-start.2
  2.3 2.8 gather_fusion
  5.2 2.8 gather_fusion.1
  8.3 0.6 stack.46.small
  8.9 147.4 %forward_exchange.1 = (bf16[4,32,8,1024]{3,2,1,0:T(8,128)(2,1)}, bf16[1024,1024]{1,0:T(8,128)(2,1)}, bf16[1024,1024]{1,0:T(8,128)(2,1)}, bf16[1024,1024]{1,0:T(8...) custom-call(bf16[16,4,8,1024]{3,2,1,0:T(8,128)(2,1)} %bitcast.33, ...), custom_call_target="tpu_custom_call" | custom-call | tf_op jit(solution)/shard_map/forward_exchange/pallas_call | solution.py:732
  156.3 49.5 %middle_exchange.1 = (f32[4,128,1024]{2,1,0:T(8,128)}, bf16[4,2,128,512]{3,2,1,0:T(8,128)(2,1)}, bf16[4,2,64,2048]{3,2,1,0:T(8,128)(2,1)}, bf16[16,64,1024]{2,1,...) custom-call(bf16[1024,2048]{1,0:T(8,128)(2,1)} %get-tuple-element.45, ...), custom_call_target="tpu_custom_call" | custom-call | tf_op jit(solution)/shard_map/middle_exchange/pallas_call | solution.py:1052
  205.8 116.9 %backward_exchange.1 = (bf16[16,4,8,1024]{3,2,1,0:T(8,128)(2,1)}, bf16[16,4,8,1024]{3,2,1,0:T(8,128)(2,1)}, f32[64,3072]{1,0:T(8,128)}, f32[64,1024]{1,0:T(8,128...) custom-call(bf16[12,1024,128]{2,1,0:T(8,128)(2,1)} %get-tuple-element.44.qkv, ...), custom_call_target="tpu_custom_call" | custom-call | tf_op jit(solution)/shard_map/backward_exchange/pallas_call | solution.py:1362
  322.7 0.1 select_reduce_fusion
  322.8 4.2 %gather_fusion.2 = bf16[512,1024]{1,0:T(8,128)(2,1)S(1)} fusion(bf16[512,1024]{1,0:T(8,128)(2,1)} %bitcast.31, s32[1024]{0:T(1024)S(1)} %pad_clamp_fusion), kind=kCustom, calls=%fused_computation.2 | custom fusion | bytes 2099200 | tf_op jit(solution)/shard_map/jit(_take)/gather | solution.py:1428
  327.0 2.1 gather_fusion.3
  329.0 0.7 iota_compare_fusion.3
  329.7 1.5 bitcast_select_fusion
  331.3 0.5 slice_bitcast_fusion
  331.8 0.6 slice.30
  332.4 0.5 slice_bitcast_fusion.4
  332.9 0.9 copy.34
  333.8 0.7 copy.35
  334.5 1.0 copy.36
  335.5 1.0 copy.37
  (52 shorter events, 0.2 us)
Async XLA Ops:
  0.6 1.7 copy-start
  2.3 2.8 copy-start.2
  5.1 2.9 copy-start.9
  5.1 2.9 copy-start.10
  5.1 2.9 copy-start.11
  5.1 2.9 copy-start.12
  5.2 3.0 copy-start.13
  5.2 3.0 copy-start.14
  5.2 3.0 copy-start.15
  5.2 3.0 copy-start.16
  322.8 4.2 %copy-start.3 = (bf16[16,4,8,1024]{3,2,1,0:T(8,128)(2,1)S(1)}, bf16[16,4,8,1024]{3,2,1,0:T(8,128)(2,1)}, u32[]{:S(2)}) copy-start(bf16[16,4,8,1024]{3,2,1,0:T(8,128)(2,1)} %get-tuple-element.68) | copy-start | bytes 3145732
  329.7 1.6 copy-start.8
  329.7 3.2 copy-start.6
  329.7 4.0 %copy-start.7 = (f32[64,1024]{1,0:T(8,128)S(1)}, f32[64,1024]{1,0:T(8,128)}, u32[]{:S(2)}) copy-start(f32[64,1024]{1,0:T(8,128)} %get-tuple-element.104) | copy-start | bytes 786436
  331.3 3.2 copy-start.5
  332.9 2.6 copy-start.4
  333.8 2.7 copy-start.1

commit v2 on v1

--- a/solution.py
+++ b/solution.py
@@ -1066,7 +1066,7 @@
     qkv, do, n1, qkvw, x_all, dh2, keep, give, ry2, rc1, wd, smalls, vec, slopes,
     ret_y, ret_x, o_qkv, o_dense, o_up, o_down, o_small,
     qkv_v, do_v, dqkv_v, n1_v, qkvw_v, x_v, dh2_v, dk_acc, dv_acc, bias_acc, mine_v, sent_v, got_v, dx_v, gq_v,
-    small_v, small_got, small_fin, small_last, f_qkv, f_dense, f_up, f_down, keep_v, give_v, y_v, own_wd, idc, idr,
+    small_v, small_got, small_fin, small_last, f_qkv, f_dense, f_up, f_down, keep_v, give_v, y_v, own_wd, idc, idr, zero_v,
     *rest,
 ):
     bufs, (send_sems, recv_sems, copy_sems) = rest[:-3], rest[-3:]
@@ -1110,6 +1110,7 @@
         bring(smalls, small_v),
     ]
     enter(g)
+    zero_v[...] = jnp.zeros_like(zero_v)
     idc[...] = blocked_ids(idc.shape, 0, lanes)
     idr[...] = blocked_ids(idr.shape, 1, lanes)
     rc_in.wait()
@@ -1274,6 +1275,7 @@
         small_v[j, 0:1, :rows] = gains[:, j * rows : (j + 1) * rows]
         small_v[j, 1:2, :rows] = biases[:, j * rows : (j + 1) * rows]
     kept = [own_y, bring(dx_v.at[:, g.k], ret_x.at[g.k])]
+    kept += [bring(zero_v, ret_y.at[shards]), bring(zero_v, ret_x.at[shards])]
     for d in range(1, shards):
         to = (g.k + d) % shards
         wires.send(small_v.at[to], small_got.at[g.k], small_at + d, g.s, to, small_v.at[0])
@@ -1339,7 +1341,7 @@
     counts = (256, 48)
     cut = lambda a: a.reshape((4, 2, 2) + a.shape[1:])
     any_, vmem = pl.BlockSpec(memory_space=pl.ANY), pl.BlockSpec(memory_space=pltpu.VMEM)
-    ret = (shards, blocks, ROWS, width)
+    ret = (shards + 1, blocks, ROWS, width)
     outs = [
         (ret, bf16), (ret, bf16), ((rows, 3 * width), f32), ((rows, width), f32), ((rows, seqs * ff), f32),
         ((seqs * ff_part, width), f32), (smalls.shape[1:], f32),
@@ -1354,7 +1356,7 @@
         ((2,) + smalls.shape[1:], f32), (smalls.shape[1:], f32), ((rows, 3 * width), f32), ((rows, width), f32), ((rows, seqs * ff), f32),
         ((seqs * ff_part, width), f32), ((blocks, half, width), f32), ((blocks, half, width), bf16),
         ((blocks, shards, ROWS, width), bf16), ((4, 2) + blks[2], bf16),
-        ((tokens, 1), f32), ((1, tokens), f32),
+        ((tokens, 1), f32), ((1, tokens), f32), ((blocks, ROWS, width), bf16),
     ]
     for blk in blks:
         scratch += [((4, 2) + blk, bf16)] * (blk is not blks[0])
@@ -1421,12 +1423,11 @@
 
     row_here = jnp.arange(slots, dtype=jnp.int32)[:, None]
     inside = (row_here >= row_start[None]) & (row_here < (row_start + seq_rows)[None])
-    fetch = jnp.sum(jnp.where(inside, number[None] * rows + row_here - row_start[None], 0), axis=1)
-    fetch_live = jnp.arange(slots, dtype=jnp.int32) < jnp.sum(seq_rows)
+    fetch = jnp.sum(jnp.where(inside, number[None] * rows + row_here - row_start[None] - shards * rows, 0), axis=1)
+    fetch = fetch + shards * rows
 
     def to_stream(got):
-        taken = jnp.take(got.reshape(-1, width), fetch, axis=0, mode="clip")
-        return jnp.where(fetch_live[:, None], taken, jnp.zeros_like(taken))[None]
+        return jnp.take(got.reshape(-1, width), fetch, axis=0, mode="clip")[None]
 
     vectors_out = tuple(g_small[i, : a.shape[0]] for i, a in enumerate(smalls_in))
     g_gain_one, g_bias_one, g_qv, g_bdense, g_gain_two, g_bias_two, g_bup, g_bdown = vectors_out

time: 337 us -> 336 us (level)
  no operation moved by 1% of the time
where the time goes in v2:
time: 336 us; the launch traced here: 335 us
  Pallas kernels  314 us (93%)
  local copies, waits for them, and re-layouts  18.9 us (6%)
    pallas_call x1, Pallas kernels, forward_exchange(): pl.pallas_call(functools.partial(forward_kernel, seqs, shards, counts), i...  147 us
    pallas_call x1, Pallas kernels, backward_exchange(): pl.pallas_call(functools.partial(backward_kernel, seqs, shards, counts),...  117 us
    pallas_call x1, Pallas kernels, middle_exchange(): pl.pallas_call(functools.partial(middle_kernel, seqs, shards, counts), in...  49.5 us
    gather x2, local copies, waits for them, and re-layouts, to_stream(): return jnp.take(got.reshape(-1, width), fetch, axis=0, mode='clip')[None]  7.73 us

profile of v2, /device:TPU:0, one launch (start us, length us, event | category | flops | bytes accessed | tf_op | source)
XLA Modules:
  0.0 335.3 jit_solution(5539301120137257400)
XLA Ops:
  0.6 0.0 copy-start
  0.7 0.8 and_select_fusion
  1.4 0.1 select_reduce_fusion.1
  1.5 0.1 iota_add_fusion
  1.6 0.1 reshape.100
  1.7 0.2 copy-done
  1.9 2.8 gather_fusion
  4.7 0.0 copy-start.14
  4.7 0.0 copy-start.15
  4.7 2.8 gather_fusion.1
  7.8 0.6 stack.46.small
  8.4 147.4 %forward_exchange.1 = (bf16[4,32,8,1024]{3,2,1,0:T(8,128)(2,1)}, bf16[1024,1024]{1,0:T(8,128)(2,1)}, bf16[1024,1024]{1,0:T(8,128)(2,1)}, bf16[1024,1024]{1,0:T(8...) custom-call(bf16[16,4,8,1024]{3,2,1,0:T(8,128)(2,1)} %bitcast.31, ...), custom_call_target="tpu_custom_call" | custom-call | tf_op jit(solution)/shard_map/forward_exchange/pallas_call | solution.py:732
  155.8 49.5 %middle_exchange.1 = (f32[4,128,1024]{2,1,0:T(8,128)}, bf16[4,2,128,512]{3,2,1,0:T(8,128)(2,1)}, bf16[4,2,64,2048]{3,2,1,0:T(8,128)(2,1)}, bf16[16,64,1024]{2,1,...) custom-call(bf16[1024,2048]{1,0:T(8,128)(2,1)} %get-tuple-element.45, ...), custom_call_target="tpu_custom_call" | custom-call | tf_op jit(solution)/shard_map/middle_exchange/pallas_call | solution.py:1052
  205.3 116.8 %backward_exchange.1 = (bf16[17,4,8,1024]{3,2,1,0:T(8,128)(2,1)}, bf16[17,4,8,1024]{3,2,1,0:T(8,128)(2,1)}, f32[64,3072]{1,0:T(8,128)}, f32[64,1024]{1,0:T(8,128...) custom-call(bf16[12,1024,128]{2,1,0:T(8,128)(2,1)} %get-tuple-element.44.qkv, ...), custom_call_target="tpu_custom_call" | custom-call | tf_op jit(solution)/shard_map/backward_exchange/pallas_call | solution.py:1364
  322.2 0.1 select_reduce_fusion
  322.3 5.0 %gather_fusion.3 = bf16[512,1024]{1,0:T(8,128)(2,1)} fusion(bf16[544,1024]{1,0:T(8,128)(2,1)} %bitcast.29, s32[1024]{0:T(1024)S(1)} %pad_clamp_fusion), kind=kCustom, calls=%fused_computation.3 | custom fusion | bytes 2099200 | tf_op jit(solution)/shard_map/jit(_take)/gather | solution.py:1430
  327.3 2.8 gather_fusion.2
  330.1 0.5 slice_bitcast_fusion
  330.6 0.6 slice.30
  331.2 0.5 slice_bitcast_fusion.4
  331.7 0.9 copy.34
  332.6 0.7 copy.35
  333.3 1.0 copy.36
  334.3 1.0 copy.37
  (53 shorter events, 0.2 us)
Async XLA Ops:
  0.6 1.2 copy-start
  1.9 2.8 copy-start.2
  4.7 2.9 copy-start.10
  4.7 2.9 copy-start.11
  4.7 2.9 copy-start.12
  4.7 2.9 copy-start.13
  4.7 3.0 copy-start.14
  4.7 3.0 copy-start.15
  4.7 3.0 copy-start.16
  4.7 3.0 copy-start.17
  205.3 116.9 %copy-start.9 = (s32[16]{0:T(128)S(1)}, s32[16]{0:T(128)}, u32[]{:S(2)}) copy-start(s32[16]{0:T(128)} %lengths.1) | copy-start | bytes 196
  322.3 5.0 %copy-start.3 = (bf16[17,4,8,1024]{3,2,1,0:T(8,128)(2,1)S(1)}, bf16[17,4,8,1024]{3,2,1,0:T(8,128)(2,1)}, u32[]{:S(2)}) copy-start(bf16[17,4,8,1024]{3,2,1,0:T(8,128)(2,1)} %get-tuple-element.67) | copy-start | bytes 3342340
  327.3 2.8 copy-start.8
  327.3 4.4 %copy-start.6 = (f32[64,3072]{1,0:T(8,128)S(1)}, f32[64,3072]{1,0:T(8,128)}, u32[]{:S(2)}) copy-start(f32[64,3072]{1,0:T(8,128)} %get-tuple-element.98) | copy-start | bytes 2359300
  327.3 5.3 %copy-start.7 = (f32[64,1024]{1,0:T(8,128)S(1)}, f32[64,1024]{1,0:T(8,128)}, u32[]{:S(2)}) copy-start(f32[64,1024]{1,0:T(8,128)} %get-tuple-element.100) | copy-start | bytes 786436
  330.1 3.2 copy-start.5
  331.7 2.6 copy-start.4
  332.6 2.7 copy-start.1

commit v3 on v2

--- a/solution.py
+++ b/solution.py
@@ -516,6 +516,11 @@
     idr[...] = blocked_ids(idr.shape, 1, lanes)
     for made in staged_qkv:
         made.wait()
+    smalls = Smalls(wires, small_v, smalls_at)
+    qkv_all.start()
+    qkv_all.start_near()
+    tokens.start(0)
+    tokens.start(1)
     staged_small.wait()
     staged_dense.wait()
     for made in staged_up:
@@ -524,11 +529,6 @@
     staged_x.wait()
     staged_cot.wait()
     kept = [bring(fc2_v, fc2_out.at[g.k])]
-    smalls = Smalls(wires, small_v, smalls_at)
-    qkv_all.start()
-    qkv_all.start_near()
-    tokens.start(0)
-    tokens.start(1)
     smalls.start()
     dense_all.start_near()
     up_all.start_near()

time: 336 us -> 336 us (level)
  no operation moved by 1% of the time
where the time goes in v3:
time: 336 us; the launch traced here: 335 us
  Pallas kernels  314 us (93%)
  local copies, waits for them, and re-layouts  18.9 us (6%)
    pallas_call x1, Pallas kernels, forward_exchange(): pl.pallas_call(functools.partial(forward_kernel, seqs, shards, counts), i...  147 us
    pallas_call x1, Pallas kernels, backward_exchange(): pl.pallas_call(functools.partial(backward_kernel, seqs, shards, counts),...  117 us
    pallas_call x1, Pallas kernels, middle_exchange(): pl.pallas_call(functools.partial(middle_kernel, seqs, shards, counts), in...  49.6 us
    gather x2, local copies, waits for them, and re-layouts, to_stream(): return jnp.take(got.reshape(-1, width), fetch, axis=0, mode='clip')[None]  7.73 us

profile of v3, /device:TPU:0, one launch (start us, length us, event | category | flops | bytes accessed | tf_op | source)
XLA Modules:
  0.0 335.2 jit_solution(2798105844295455033)
XLA Ops:
  0.6 0.0 copy-start
  0.7 0.8 and_select_fusion
  1.4 0.1 select_reduce_fusion.1
  1.5 0.1 iota_add_fusion
  1.6 0.1 reshape.100
  1.7 0.2 copy-done
  1.9 2.8 gather_fusion
  4.7 0.0 copy-start.14
  4.7 0.0 copy-start.15
  4.7 2.8 gather_fusion.1
  7.8 0.6 stack.46.small
  8.4 147.2 %forward_exchange.1 = (bf16[4,32,8,1024]{3,2,1,0:T(8,128)(2,1)}, bf16[1024,1024]{1,0:T(8,128)(2,1)}, bf16[1024,1024]{1,0:T(8,128)(2,1)}, bf16[1024,1024]{1,0:T(8...) custom-call(bf16[16,4,8,1024]{3,2,1,0:T(8,128)(2,1)} %bitcast.31, ...), custom_call_target="tpu_custom_call" | custom-call | tf_op jit(solution)/shard_map/forward_exchange/pallas_call | solution.py:732
  155.6 49.6 %middle_exchange.1 = (f32[4,128,1024]{2,1,0:T(8,128)}, bf16[4,2,128,512]{3,2,1,0:T(8,128)(2,1)}, bf16[4,2,64,2048]{3,2,1,0:T(8,128)(2,1)}, bf16[16,64,1024]{2,1,...) custom-call(bf16[1024,2048]{1,0:T(8,128)(2,1)} %get-tuple-element.45, ...), custom_call_target="tpu_custom_call" | custom-call | tf_op jit(solution)/shard_map/middle_exchange/pallas_call | solution.py:1052
  205.3 116.8 %backward_exchange.1 = (bf16[17,4,8,1024]{3,2,1,0:T(8,128)(2,1)}, bf16[17,4,8,1024]{3,2,1,0:T(8,128)(2,1)}, f32[64,3072]{1,0:T(8,128)}, f32[64,1024]{1,0:T(8,128...) custom-call(bf16[12,1024,128]{2,1,0:T(8,128)(2,1)} %get-tuple-element.44.qkv, ...), custom_call_target="tpu_custom_call" | custom-call | tf_op jit(solution)/shard_map/backward_exchange/pallas_call | solution.py:1364
  322.2 0.1 select_reduce_fusion
  322.3 5.0 %gather_fusion.3 = bf16[512,1024]{1,0:T(8,128)(2,1)} fusion(bf16[544,1024]{1,0:T(8,128)(2,1)} %bitcast.29, s32[1024]{0:T(1024)S(1)} %pad_clamp_fusion), kind=kCustom, calls=%fused_computation.3 | custom fusion | bytes 2099200 | tf_op jit(solution)/shard_map/jit(_take)/gather | solution.py:1430
  327.3 2.8 gather_fusion.2
  330.1 0.5 slice_bitcast_fusion
  330.6 0.6 slice.30
  331.2 0.5 slice_bitcast_fusion.4
  331.7 0.9 copy.34
  332.6 0.7 copy.35
  333.3 1.0 copy.36
  334.2 1.0 copy.37
  (53 shorter events, 0.2 us)
Async XLA Ops:
  0.6 1.2 copy-start
  1.9 2.8 copy-start.2
  4.7 2.9 copy-start.10
  4.7 2.9 copy-start.11
  4.7 2.9 copy-start.12
  4.7 2.9 copy-start.13
  4.7 3.0 copy-start.14
  4.7 3.0 copy-start.15
  4.7 3.0 copy-start.16
  4.7 3.0 copy-start.17
  205.3 116.9 %copy-start.9 = (s32[16]{0:T(128)S(1)}, s32[16]{0:T(128)}, u32[]{:S(2)}) copy-start(s32[16]{0:T(128)} %lengths.1) | copy-start | bytes 196
  322.3 5.0 %copy-start.3 = (bf16[17,4,8,1024]{3,2,1,0:T(8,128)(2,1)S(1)}, bf16[17,4,8,1024]{3,2,1,0:T(8,128)(2,1)}, u32[]{:S(2)}) copy-start(bf16[17,4,8,1024]{3,2,1,0:T(8,128)(2,1)} %get-tuple-element.67) | copy-start | bytes 3342340
  327.3 2.8 copy-start.8
  327.3 4.4 %copy-start.6 = (f32[64,3072]{1,0:T(8,128)S(1)}, f32[64,3072]{1,0:T(8,128)}, u32[]{:S(2)}) copy-start(f32[64,3072]{1,0:T(8,128)} %get-tuple-element.98) | copy-start | bytes 2359300
  327.3 5.3 %copy-start.7 = (f32[64,1024]{1,0:T(8,128)S(1)}, f32[64,1024]{1,0:T(8,128)}, u32[]{:S(2)}) copy-start(f32[64,1024]{1,0:T(8,128)} %get-tuple-element.100) | copy-start | bytes 786436
  330.1 3.2 copy-start.5
  331.7 2.6 copy-start.4
  332.6 2.7 copy-start.1
